TPU v7x, 256 devices: a whole 4x4x8 slice. The times are simulated.
256 devices in a mesh: grp: 64 (over y, x, z_lo, core), con: 4 (over z_hi).
Axes of the slice: x: 4, y: 4, z: 8 (z_hi: 4, z_lo: 2; z = z_hi * 2 + z_lo), core: 2. Of those that a mesh axis runs over, the one named last changes fastest.
Arguments:
- amplitudes: bfloat16 [1600, 384, 384], P('grp', None, 'con'), may hold values from -6 to 6
- integrals: bfloat16 [40, 384, 3, 384], P(None, 'con'), may hold values from -0.046875 to 0.046875
- occ_energy: float32 [40], replicated, may hold values from -2 to -0.5
- vir_energy: float32 [384], replicated, may hold values from 0.2 to 3
- occ_irrep: int32 [40], replicated, may hold values from 0 to 7
- vir_irrep: int32 [384], replicated, may hold values from 0 to 7, as said below
Outputs:
- update: float32 [40, 3, 384, 384], P('con', None, 'grp')
Inputs may be any that keep to these rules, and one draw needn't show every extreme that they name: `occ_irrep`: D2h labels as 3-bit numbers; the product of two irreducible representations is the exclusive or of their labels. `vir_irrep`: D2h labels as 3-bit numbers; at most 192 virtual orbitals share one label, and some label is shared by exactly that many.
All inputs are finite; a program needn't handle non-finite values.
Results may differ from a plain program's by a relative error of at most 0.0031.
Values may be sent and summed in bfloat16 or wider, within the bound.
No kernel may reach another device: no remote copies, remote signals or barrier semaphores. Data moves between devices by JAX's collectives and lax.ppermute only.
A program may use at most 128 MiB of HBM per device.

v0:
```python
import jax
import jax.numpy as jnp
from jax import lax
from jax.sharding import PartitionSpec as P

OCC = 40
VIR = 384
OJW = 3


def in_blocks(x, dim, peers):
    shape = x.shape
    parts = x.reshape(*shape[:dim], peers, shape[dim] // peers, *shape[dim + 1 :])
    return jnp.moveaxis(parts, dim, 0)


def sum_at_owner(x, axis, dim):
    parts = in_blocks(x, dim, lax.axis_size(axis))
    arrived = lax.all_to_all(parts, axis, split_axis=0, concat_axis=0, tiled=True)
    return arrived.sum(axis=0)


def combine_pairs(direct, crossed):
    return (2.0 * direct.astype(jnp.float32) - crossed.astype(jnp.float32)).astype(jnp.bfloat16)


def shards(amplitudes, integrals, occ_energy, vir_energy, occ_irrep, vir_irrep):
    groups = lax.axis_size("grp")
    pair_local = amplitudes.shape[0]
    slice_width = amplitudes.shape[2]
    sectioned = amplitudes.reshape(pair_local, groups, VIR // groups, slice_width)
    received = lax.all_to_all(sectioned, "grp", split_axis=1, concat_axis=0, tiled=True)
    pair_block = received.reshape(OCC, OCC, received.shape[2], received.shape[3])
    combined = combine_pairs(pair_block, jnp.swapaxes(pair_block, 0, 1))
    partial_value = jnp.einsum(
        "ikac,kcjb->ijab", combined, integrals, preferred_element_type=jnp.float32
    )
    cycle_term = sum_at_owner(partial_value, "con", 0)
    occ_local = cycle_term.shape[0]
    vir_local = cycle_term.shape[2]
    occ_first = lax.axis_index("con") * occ_local
    vir_first = lax.axis_index("grp") * vir_local
    energy_i = lax.dynamic_slice_in_dim(occ_energy, occ_first, occ_local, 0)
    energy_a = lax.dynamic_slice_in_dim(vir_energy, vir_first, vir_local, 0)
    label_i = lax.dynamic_slice_in_dim(occ_irrep, occ_first, occ_local, 0)
    label_a = lax.dynamic_slice_in_dim(vir_irrep, vir_first, vir_local, 0)
    denominator = (
        energy_i[:, None, None, None]
        + occ_energy[:OJW][None, :, None, None]
        - energy_a[None, None, :, None]
        - vir_energy[None, None, None, :]
    )
    label = jnp.bitwise_xor(label_i[:, None, None, None], occ_irrep[:OJW][None, :, None, None])
    label = jnp.bitwise_xor(label, label_a[None, None, :, None])
    label = jnp.bitwise_xor(label, vir_irrep[None, None, None, :])
    symmetric = (label == 0).astype(jnp.float32)
    return symmetric * cycle_term / denominator


def solution(mesh):
    return jax.shard_map(
        shards,
        mesh=mesh,
        in_specs=(P("grp", None, "con"), P(None, "con", None, None), P(), P(), P(), P()),
        out_specs=P("con", None, "grp", None),
        check_vma=False,
    )
```

profile of v0, /device:TPU:1, one launch (start us, length us, event | category | flops | bytes accessed | tf_op | source)
XLA Modules:
  0.0 132.1 jit_solution(10573091456133046015)
XLA Ops:
  0.0 4.7 %copy.26 = bf16[25,384,96]{2,0,1:T(8,128)(2,1)} copy(bf16[25,384,96]{1,2,0:T(8,128)(2,1)} %param.6) | data formatting | bytes 3686400 | tf_op jit(solution)/shard_map/reshape | solution.py:31
  4.7 51.1 %all_to_all.14 = bf16[25,64,6,96]{3,0,2,1:T(8,128)(2,1)S(1)} all-to-all(bf16[25,64,6,96]{3,0,2,1:T(8,128)(2,1)} %bitcast.34), channel_id=1, replica_groups=mesh['grp'=64,'con'=4] {'grp'}, dimensions={1} | all-to-all | bytes 3686400 | tf_op jit(solution)/shard_map/all_to_all | solution.py:32
  55.8 0.9 fusion.3
  56.8 3.4 %copy.18 = f32[64,25,1,6,96]{4,1,0,3,2:T(8,128)} copy(f32[64,25,1,6,96]{4,1,3,0,2:T(8,128)S(1)} %fusion.3) | data formatting | bytes 7372800 | tf_op jit(solution)/shard_map/mul | solution.py:24
  60.1 6.6 %mul.26 = f32[40,40,6,96]{3,1,0,2:T(8,128)} reshape(f32[64,25,1,6,96]{4,1,0,3,2:T(8,128)} %copy.18) | data formatting | bytes 7372800 | tf_op jit(solution)/shard_map/mul | solution.py:24
  66.7 0.9 convert_bitcast_fusion
  67.6 3.4 %copy.19 = f32[64,25,1,6,96]{4,1,0,3,2:T(8,128)} copy(f32[64,25,1,6,96]{4,1,3,0,2:T(8,128)S(1)} %convert_bitcast_fusion) | data formatting | bytes 7372800 | tf_op jit(solution)/shard_map/convert_element_type | solution.py:24
  70.9 6.6 %reshape.99 = f32[40,40,6,96]{3,1,0,2:T(8,128)} reshape(f32[64,25,1,6,96]{4,1,0,3,2:T(8,128)} %copy.19) | data formatting | bytes 7372800 | tf_op jit(solution)/shard_map/convert_element_type | solution.py:24
  77.6 5.0 %fusion.5 = bf16[40,40,6,96,1]{3,1,0,2,4:T(8,128)(2,1)S(1)} fusion(f32[40,40,6,96]{3,1,0,2:T(8,128)} %mul.26, f32[40,40,6,96]{3,1,0,2:T(8,128)} %reshape.99), kind=kLoop, calls=%fused_computation.8 | loop fusion | flops 1843200 | bytes 9216000 | tf_op jit(solution)/shard_map/convert_element_type | solution.py:24
  82.5 5.7 %fusion.7 = f32[40,3,6,384]{3,0,1,2:T(8,128)S(1)} fusion(bf16[40,96,3,384]{3,1,2,0:T(8,128)(2,1)} %param.7, bf16[40,40,6,96,1]{3,1,0,2,4:T(8,128)(2,1)S(1)} %fusion.5), kind=kOutput, calls=%fused_computation.10 | convolution fusion | flops 2123366400 | bytes 11796480 | tf_op jit(solution)/shard_map/ikac,kcjb->ijab/dot_general | solution.py:35
  88.2 0.0 copy-start
  88.3 0.0 copy-start.1
  88.3 0.0 copy-start.2
  88.3 0.0 copy-start.3
  88.3 1.4 %copy.23 = f32[40,3,6,384]{3,2,1,0:T(8,128)} copy(f32[40,3,6,384]{3,0,1,2:T(8,128)S(1)} %fusion.7) | data formatting | bytes 2211840 | tf_op jit(solution)/shard_map/ikac,kcjb->ijab/transpose | solution.py:35
  89.7 7.3 %all-to-all-start.1 = ((f32[4,10,3,6,384]{4,3,2,1,0:T(8,128)}), f32[4,10,3,6,384]{4,3,2,1,0:T(8,128)S(1)}, u32[]{:S(2)}, u32[]{:S(2)}) async-start(f32[4,10,3,6,384]{4,3,2,1,0:T(8,128)} %bitcast.11), calls=%async_computation.1 | async-start | bytes 2949120 | tf_op jit(solution)/shard_map/all_to_all | solution.py:19
  97.0 0.0 copy-done
  97.0 0.1 dynamic_slice.15
  97.0 0.0 copy-done.1
  97.0 0.1 dynamic_slice.13
  97.1 0.0 copy-done.2
  97.1 0.1 dynamic_slice.14
  97.2 0.0 copy-done.3
  97.2 0.1 dynamic_slice.12
  97.3 0.1 broadcast_add_fusion
  97.3 0.1 broadcast_xor_fusion.1
  97.4 0.1 broadcast_subtract_fusion
  97.5 0.1 broadcast_xor_fusion
  97.6 33.5 %all-to-all-done.1 = f32[4,10,3,6,384]{4,3,2,1,0:T(8,128)S(1)} async-done(((f32[4,10,3,6,384]{4,3,2,1,0:T(8,128)}), f32[4,10,3,6,384]{4,3,2,1,0:T(8,128)S(1)}, u32[]{:S(2)}, u32[]{:S(2)}) %all-to-all-start.1) | async-done | bytes 1105952 | tf_op jit(solution)/shard_map/all_to_all | solution.py:19
  131.1 0.1 reduce_sum.9
  131.2 0.9 subtract_divide_fusion
Async XLA Ops:
  88.2 8.7 %copy-start = (f32[384]{0:T(512)S(1)}, f32[384]{0:T(512)}, u32[]{:S(2)}) copy-start(f32[384]{0:T(512)} %param.9) | copy-start | bytes 4612
  88.3 8.8 %copy-start.1 = (s32[384]{0:T(512)S(1)}, s32[384]{0:T(512)}, u32[]{:S(2)}) copy-start(s32[384]{0:T(512)} %param.11) | copy-start | bytes 4612
  88.3 8.9 %copy-start.2 = (f32[40]{0:T(128)S(1)}, f32[40]{0:T(128)}, u32[]{:S(2)}) copy-start(f32[40]{0:T(128)} %param.8) | copy-start | bytes 484
  88.3 8.9 %copy-start.3 = (s32[40]{0:T(128)S(1)}, s32[40]{0:T(128)}, u32[]{:S(2)}) copy-start(s32[40]{0:T(128)} %param.10) | copy-start | bytes 484
  89.7 41.4 %all-to-all-start.1 = ((f32[4,10,3,6,384]{4,3,2,1,0:T(8,128)}), f32[4,10,3,6,384]{4,3,2,1,0:T(8,128)S(1)}, u32[]{:S(2)}, u32[]{:S(2)}) async-start(f32[4,10,3,6,384]{4,3,2,1,0:T(8,128)} %bitcast.11), calls=%async_computation.1 | async-start | bytes 2949120 | tf_op jit(solution)/shard_map/all_to_all | solution.py:19
where the time goes:
time: 133 us; the launch traced here: 132 us
  blocking collectives  51.1 us (38%)
  waiting for transfers between devices  33.5 us (25%)
  local copies, waits for them, and re-layouts  26.3 us (20%)
  other arithmetic  8.08 us (6%)
  starting transfers between devices  7.27 us (5%)
  matrix products  5.73 us (4%)
    all_to_all x1, blocking collectives, shards(): lax.all_to_all(sectioned, 'grp', split_axis=1, concat_axis=0, tiled=True)  51.1 us
    all_to_all x1, waiting for transfers between devices, sum_at_owner(): lax.all_to_all(parts, axis, split_axis=0, concat_axis=0, tiled=True)  33.5 us
    convert_element_type x2, local copies, waits for them, and re-layouts, combine_pairs(): crossed.astype(jnp.float32)  9.96 us
    mul x2, local copies, waits for them, and re-layouts, combine_pairs(): 2.0 * direct.astype(jnp.float32) - crossed.astype(jnp.float32)  9.91 us
    all_to_all x1, starting transfers between devices, sum_at_owner(): lax.all_to_all(parts, axis, split_axis=0, concat_axis=0, tiled=True)  7.27 us
    dot_general x1, matrix products, shards(): jnp.einsum('ikac,kcjb->ijab', combined, integrals, preferred_element_type...  5.73 us
    convert_element_type x1, other arithmetic, combine_pairs(): (2.0 * direct.astype(jnp.float32) - crossed.astype(jnp.float32)).astype(j...  4.96 us
    reshape x1, local copies, waits for them, and re-layouts, shards(): amplitudes.reshape(pair_local, groups, VIR // groups, slice_width)  4.74 us
  transfers between devices with their start and end apart: 1, of which 1 were waited for; matrix products, arithmetic and copies ran while one was open for 0% of the time, Pallas kernels for 0%

commit v1 on v0

v1 whole, which is shorter than its diff:
```python
import functools

import jax
import jax.numpy as jnp
from jax import lax
from jax.experimental import pallas as pl
from jax.experimental.pallas import tpu as pltpu
from jax.sharding import PartitionSpec as P

OCC = 40
VIR = 384
OJW = 3
GRP = 64
CON = 4
PAIR = OCC * OCC // GRP
SEC = VIR // GRP
CW = VIR // CON
OWN = OCC // CON
SLOT = VIR // 2
TILES = 19
MSG = 120
VMEM = pl.BlockSpec(memory_space=pltpu.VMEM)
SMEM = pl.BlockSpec(memory_space=pltpu.SMEM)
HBM = pl.BlockSpec(memory_space=pl.ANY)
LIMIT = 56 * 1024 * 1024


def nt_dot(x, y):
    return lax.dot_general(x, y, (((1,), (1,)), ((), ())), preferred_element_type=jnp.float32)


def pack_kernel(x_ref, out_ref, main_ref, rest_ref):
    for t in range(TILES):
        group, j = divmod(t, 4)
        quad, q = divmod(t, 3)
        if j < 3:
            dst, at = main_ref.at[j], group * 128
        else:
            dst, at = rest_ref, group * 128
        dst[at : at + 96, :] = x_ref[4 * quad + q]
        if 4 * quad + 3 < PAIR:
            dst[at + 96 : at + 128, :] = x_ref[4 * quad + 3, 32 * q : 32 * q + 32, :]
        else:
            dst[at + 96 : at + 128, :] = jnp.zeros((32, VIR), jnp.bfloat16)
    row = lax.broadcasted_iota(jnp.int32, (GRP * 8, VIR), 0)
    col = lax.broadcasted_iota(jnp.int32, (GRP * 8, VIR), 1)
    dest, sub = row // 8, row % 8
    pick = jnp.where((sub < 6) & (col == dest * 6 + sub), 1.0, 0.0).astype(jnp.bfloat16)
    for j in range(3):
        pick_rest = jnp.where((sub >= 6) & (col == dest * 6 + 2 * j + sub - 6), 1.0, 0.0).astype(jnp.bfloat16)
        main = nt_dot(pick, main_ref[j])
        rest = nt_dot(pick_rest, rest_ref[...])
        for group in range(5):
            tile = main[:, group * 128 : group * 128 + 128]
            if group < 4:
                tile = tile + rest[:, group * 128 : group * 128 + 128]
            at = (group * 3 + j) * 8
            out_ref[:, at : at + 8, :] = tile.astype(jnp.bfloat16).reshape(GRP, 8, 128)


def pack(x):
    return pl.pallas_call(
        pack_kernel,
        out_shape=jax.ShapeDtypeStruct((GRP, MSG, 128), jnp.bfloat16),
        in_specs=[VMEM],
        out_specs=VMEM,
        scratch_shapes=[
            pltpu.VMEM((3, 640, VIR), jnp.bfloat16),
            pltpu.VMEM((512, VIR), jnp.bfloat16),
        ],
        compiler_params=pltpu.CompilerParams(vmem_limit_bytes=LIMIT),
        name="pack",
    )(x)


def own_column(ref, first, dtype):
    row = lax.broadcasted_iota(jnp.int32, (8, 1), 0)
    column = jnp.zeros((8, 1), dtype)
    for a in range(SEC):
        column = jnp.where(row == a, ref[first + a], column)
    return column


def term_kernel(where_ref, occ_ref, vir_ref, label_ref, got_ref, w_hbm, *refs):
    outs, fold_ref, (pairs_ref, w_ref, lhs_ref, sum_ref, sems) = refs[:5], refs[5], refs[6:]
    me = where_ref[1]

    def fetch(kq, carry):
        for q in range(3):
            for j in range(OJW):
                at = pl.multiple_of(kq % 2 * 384, 384) + q * 128
                lanes = pl.ds(j * VIR, VIR)
                pltpu.make_async_copy(
                    w_hbm.at[4 * kq + q, j], w_ref.at[kq // 2, pl.ds(at, 96), lanes], sems.at[kq // 2]
                ).start()
                pltpu.make_async_copy(
                    w_hbm.at[4 * kq + 3, j, pl.ds(32 * q, 32)],
                    w_ref.at[kq // 2, pl.ds(at + 96, 32), lanes],
                    sems.at[kq // 2],
                ).start()
        return carry

    lax.fori_loop(0, 10, fetch, 0)

    sub = lax.broadcasted_iota(jnp.int32, (8, 128), 0)
    lane = lax.broadcasted_iota(jnp.int32, (8, 128), 1)

    def unpack(s, carry):
        got = got_ref[s].astype(jnp.float32).reshape(15, 8, 128)
        tiles = []
        for t in range(TILES):
            group, j = divmod(t, 4)
            if j < 3:
                tiles.append(got[3 * group + j])
            else:
                a, b, c = (pltpu.roll(got[3 * group + n], 2 + 2 * n, 0) for n in range(3))
                tiles.append(jnp.where(sub < 2, a, jnp.where(sub < 4, b, c)))
        for p in range(PAIR):
            quad, q = divmod(p, 4)
            if q < 3:
                value = tiles[3 * quad + q]
            else:
                a, b, c = (pltpu.roll(tiles[3 * quad + n], 32 + 32 * n, 1) for n in range(3))
                value = jnp.where(lane < 32, a, jnp.where(lane < 64, b, c))
            pairs_ref[PAIR * s + p] = value
        return carry

    lax.fori_loop(0, GRP, unpack, 0)

    lane3 = lax.broadcasted_iota(jnp.int32, (OCC, 8, 128), 2)
    by_i = pairs_ref.reshape(OCC, OCC, 8, 128)

    def combine(kq, carry):
        combined = []
        for q in range(4):
            k = 4 * kq + q
            direct, crossed = by_i[:, k], by_i[k]
            combined.append(2.0 * direct - crossed)
        for q in range(3):
            rolled = pltpu.roll(combined[3], 96 - 32 * q, 2)
            merged = jnp.where(lane3 < 96, combined[q], rolled)
            at = pl.multiple_of(kq % 2 * 384, 384) + q * 128
            lhs_ref[kq // 2, :, pl.ds(at, 128)] = merged.reshape(OCC * 8, 128).astype(jnp.bfloat16)
        return carry

    lax.fori_loop(0, 10, combine, 0)

    def multiply(b, carry):
        pltpu.make_async_copy(w_ref.at[b], w_ref.at[b], sems.at[b]).wait()
        part = jnp.dot(lhs_ref[b], w_ref[b], preferred_element_type=jnp.float32)

        @pl.when(b == 0)
        def _():
            sum_ref[...] = part

        @pl.when(b > 0)
        def _():
            sum_ref[...] += part

        return carry

    lax.fori_loop(0, 5, multiply, 0)

    labels = label_ref[...]
    label_row = labels.astype(jnp.float32)
    label_col = jnp.transpose(jnp.broadcast_to(label_row, (8, VIR)))[:, :1]
    first = lax.broadcasted_iota(jnp.int32, (VIR, VIR), 0)
    second = lax.broadcasted_iota(jnp.int32, (VIR, VIR), 1)
    ahead = (label_col < label_row) | ((label_col == label_row) & (first < second))
    rank = jnp.sum(jnp.where(ahead, 1.0, 0.0), axis=0, keepdims=True)
    slot = jnp.where(rank >= SLOT, rank - SLOT, rank).astype(jnp.int32)
    fold = jnp.where(lax.broadcasted_iota(jnp.int32, (SLOT, VIR), 0) == slot, 1.0, 0.0).astype(jnp.bfloat16)
    fold_ref[...] = fold

    label_ab = own_column(vir_ref, where_ref[0] * SEC, jnp.int32) ^ labels

    def mask(i, carry):
        rows = pl.ds(pl.multiple_of(i * 8, 8), 8)
        for j in range(OJW):
            lanes = pl.ds(j * VIR, VIR)
            keep = label_ab == (occ_ref[i] ^ occ_ref[j])
            sum_ref[rows, lanes] = jnp.where(keep, sum_ref[rows, lanes], 0.0)
        return carry

    lax.fori_loop(0, OCC, mask, 0)

    row = lax.broadcasted_iota(jnp.int32, (64, OWN * 8), 0)
    col = lax.broadcasted_iota(jnp.int32, (64, OWN * 8), 1)
    dense = jnp.where((row < OWN * SEC) & (col == row // SEC * 8 + row % SEC), 1.0, 0.0).astype(jnp.bfloat16)
    for s in range(CON):
        owner = lax.rem(me + s, CON)
        rows = pl.ds(pl.multiple_of(owner * (OWN * 8), 8), OWN * 8)
        for j in range(OJW):
            value = sum_ref[rows, j * VIR : (j + 1) * VIR]
            high = value.astype(jnp.bfloat16)
            parts = [(outs[s], high)]
            if s == 0:
                parts.append((outs[4], (value - high.astype(jnp.float32)).astype(jnp.bfloat16)))
            for out, part in parts:
                part = jnp.dot(dense, part, preferred_element_type=jnp.float32).astype(jnp.bfloat16)
                out[:, j * SLOT : (j + 1) * SLOT] = nt_dot(part, fold).astype(jnp.bfloat16)


def term(where, occ_irrep, vir_irrep, label_row, got, w):
    chunk = jax.ShapeDtypeStruct((64, OJW * SLOT), jnp.bfloat16)
    return pl.pallas_call(
        term_kernel,
        out_shape=[chunk] * 5 + [jax.ShapeDtypeStruct((SLOT, VIR), jnp.bfloat16)],
        in_specs=[SMEM, SMEM, SMEM, VMEM, VMEM, HBM],
        out_specs=[VMEM] * 6,
        scratch_shapes=[
            pltpu.VMEM((OCC * OCC, 8, 128), jnp.float32),
            pltpu.VMEM((5, 768, OJW * VIR), jnp.bfloat16),
            pltpu.VMEM((5, OCC * 8, 768), jnp.bfloat16),
            pltpu.VMEM((OCC * 8, OJW * VIR), jnp.float32),
            pltpu.SemaphoreType.DMA((5,)),
        ],
        compiler_params=pltpu.CompilerParams(vmem_limit_bytes=LIMIT),
        name="term",
    )(where, occ_irrep, vir_irrep, label_row, got, w)


def finish_kernel(where_ref, occ_ref, vir_ref, occ_e_ref, vir_e_ref, label_ref, energy_ref, fold_ref, *refs):
    chunks, out_ref = refs[:5], refs[5]
    first = where_ref[1] * OWN
    label_ab = (own_column(vir_ref, where_ref[0] * SEC, jnp.int32) ^ label_ref[...])[:SEC]
    energy_a = own_column(vir_e_ref, where_ref[0] * SEC, jnp.float32)[:SEC]
    for j in range(OJW):
        total = jnp.zeros((64, VIR), jnp.float32)
        for chunk in chunks:
            total += jnp.dot(
                chunk[:, j * SLOT : (j + 1) * SLOT], fold_ref[...], preferred_element_type=jnp.float32
            )
        for i in range(OWN):
            keep = label_ab == (occ_ref[first + i] ^ occ_ref[j])
            denominator = occ_e_ref[first + i] + occ_e_ref[j] - energy_a - energy_ref[...]
            out_ref[i, j] = jnp.where(keep, total[i * SEC : (i + 1) * SEC], 0.0) / denominator


def finish(where, occ_irrep, vir_irrep, occ_energy, vir_energy, label_row, energy_row, fold, chunks):
    return pl.pallas_call(
        finish_kernel,
        out_shape=jax.ShapeDtypeStruct((OWN, OJW, SEC, VIR), jnp.float32),
        in_specs=[SMEM] * 5 + [VMEM] * 8,
        out_specs=VMEM,
        compiler_params=pltpu.CompilerParams(vmem_limit_bytes=LIMIT),
        name="finish",
    )(where, occ_irrep, vir_irrep, occ_energy, vir_energy, label_row, energy_row, fold, *chunks)


def shards(amplitudes, integrals, occ_energy, vir_energy, occ_irrep, vir_irrep):
    where = jnp.stack([lax.axis_index("grp"), lax.axis_index("con")]).astype(jnp.int32)
    label_row, energy_row = vir_irrep.reshape(1, VIR), vir_energy.reshape(1, VIR)
    sent = pack(jnp.swapaxes(amplitudes, 1, 2))
    got = lax.all_to_all(sent, "grp", split_axis=0, concat_axis=0, tiled=True)
    *chunks, fold = term(where, occ_irrep, vir_irrep, label_row, got, jnp.swapaxes(integrals, 1, 2))
    arrived = [chunks[0], chunks[4]]
    for s in range(1, CON):
        arrived.append(lax.ppermute(chunks[s], "con", [(n, (n + s) % CON) for n in range(CON)]))
    return finish(where, occ_irrep, vir_irrep, occ_energy, vir_energy, label_row, energy_row, fold, arrived)


def solution(mesh):
    return jax.shard_map(
        shards,
        mesh=mesh,
        in_specs=(P("grp", None, "con"), P(None, "con", None, None), P(), P(), P(), P()),
        out_specs=P("con", None, "grp", None),
        check_vma=False,
    )
```

time: 133 us -> 78.9 us (0.59)
  blocking collectives: 51.1 us -> 0 us
  Pallas kernels: 0 us -> 23.9 us
  local copies, waits for them, and re-layouts: 26.3 us -> 3.13 us
  starting transfers between devices: 7.27 us -> 20.1 us
  other arithmetic: 8.08 us -> 0.58 us
  matrix products: 5.73 us -> 0 us
  waiting for transfers between devices: 33.5 us -> 30.8 us
    all_to_all x1 -> x0, blocking collectives: 51.1 us -> none  [shards(): lax.all_to_all(sectioned, 'grp', split_axis=1, concat_axis=0, tiled=True)]
    pallas_call x0 -> x3, Pallas kernels: none -> 23.9 us  [the longest x1 16.4 us: term(): pl.pallas_call(term_kernel, out_shape=[chunk] * 5 + [jax.ShapeDtypeStruct...]
    convert_element_type x2 -> x0, local copies, waits for them, and re-layouts: 9.96 us -> none  [combine_pairs(): crossed.astype(jnp.float32)]
    mul x2 -> x0, local copies, waits for them, and re-layouts: 9.91 us -> none  [combine_pairs(): 2.0 * direct.astype(jnp.float32) - crossed.astype(jnp.float32)]
    ppermute x0 -> x3, starting transfers between devices: none -> 9.67 us  [shards(): lax.ppermute(chunks[s], 'con', [(n, (n + s) % CON) for n in range(CON)])]
    all_to_all x1, waiting for transfers between devices: 33.5 us -> 27 us  [shards(): got = lax.all_to_all(sent, 'grp', split_axis=0, concat_axis=0, tiled=True)]
    convert_element_type x2 -> x0, other arithmetic: 5.87 us -> none  [the longest x1 4.96 us: combine_pairs(): (2.0 * direct.astype(jnp.float32) - crossed.astype(jnp.float32)).astype(j...]
    dot_general x1 -> x0, matrix products: 5.73 us -> none  [shards(): jnp.einsum('ikac,kcjb->ijab', combined, integrals, preferred_element_type...]
  transfers between devices with their start and end apart: 1 -> 4, of which waited for: 1 -> 2; matrix products, arithmetic and copies ran while one was open for 0% -> 2% of each run, Pallas kernels for 0% -> 0%
where the time goes in v1:
time: 78.9 us; the launch traced here: 78.6 us
  waiting for transfers between devices  30.8 us (39%)
  Pallas kernels  23.9 us (30%)
  starting transfers between devices  20.1 us (25%)
  local copies, waits for them, and re-layouts  3.13 us (4%)
    all_to_all x1, waiting for transfers between devices, shards(): got = lax.all_to_all(sent, 'grp', split_axis=0, concat_axis=0, tiled=True)  27 us
    pallas_call x1, Pallas kernels, term(): pl.pallas_call(term_kernel, out_shape=[chunk] * 5 + [jax.ShapeDtypeStruct...  16.4 us
    all_to_all x1, starting transfers between devices, shards(): got = lax.all_to_all(sent, 'grp', split_axis=0, concat_axis=0, tiled=True)  10.5 us
    ppermute x3, starting transfers between devices, shards(): lax.ppermute(chunks[s], 'con', [(n, (n + s) % CON) for n in range(CON)])  9.67 us
    pallas_call x1, Pallas kernels, pack(): pl.pallas_call(pack_kernel, out_shape=jax.ShapeDtypeStruct((GRP, MSG, 128...  4.97 us
    ppermute x3, waiting for transfers between devices, shards(): lax.ppermute(chunks[s], 'con', [(n, (n + s) % CON) for n in range(CON)])  3.82 us
    pallas_call x1, Pallas kernels, finish(): pl.pallas_call(finish_kernel, out_shape=jax.ShapeDtypeStruct((OWN, OJW, S...  2.54 us
    unnamed x12, local copies, waits for them, and re-layouts  1.97 us
  transfers between devices with their start and end apart: 4, of which 2 were waited for; matrix products, arithmetic and copies ran while one was open for 2% of the time, Pallas kernels for 0%

profile of v1, /device:TPU:1, one launch (start us, length us, event | category | flops | bytes accessed | tf_op | source)
XLA Modules:
  0.0 78.6 jit_solution(5639149722933927750)
XLA Ops:
  0.0 5.0 %pack.1 = bf16[64,120,128]{2,1,0:T(8,128)(2,1)} custom-call(bf16[25,96,384]{2,1,0:T(8,128)(2,1)} %bitcast.5), custom_call_target="tpu_custom_call" | custom-call | tf_op jit(solution)/shard_map/pack/pallas_call | solution.py:62
  5.0 0.0 copy-start.4
  5.0 10.5 %all-to-all-start = ((bf16[64,120,128]{2,1,0:T(8,128)(2,1)}), bf16[64,120,128]{2,1,0:T(8,128)(2,1)S(1)}, u32[]{:S(2)}, u32[]{:S(2)}) async-start(bf16[64,120,128]{2,1,0:T(8,128)(2,1)} %pack.1), calls=%async_computation | async-start | bytes 3932160 | tf_op jit(solution)/shard_map/all_to_all | solution.py:255
  15.4 0.0 copy-done.4
  15.5 0.6 reshape.6.label_ref
  16.0 0.6 pad_add_fusion.where_ref
  16.6 27.0 %all-to-all-done.got_ref = bf16[64,120,128]{2,1,0:T(8,128)(2,1)S(1)} async-done(((bf16[64,120,128]{2,1,0:T(8,128)(2,1)}), bf16[64,120,128]{2,1,0:T(8,128)(2,1)S(1)}, u32[]{:S(2)}, u32[]{:S(2)}) %all-to-all-start) | async-done | bytes 1966112 | tf_op jit(solution)/shard_map/all_to_all | solution.py:255
  43.6 0.0 copy-start
  43.6 1.3 %copy-done = bf16[64,120,128]{2,1,0:T(8,128)(2,1)} copy-done((bf16[64,120,128]{2,1,0:T(8,128)(2,1)}, bf16[64,120,128]{2,1,0:T(8,128)(2,1)S(1)}, u32[]{:S(2)}) %copy-start) | copy-done | bytes 1966104
  44.9 0.0 copy-start.5
  44.9 16.4 %term.1 = (bf16[64,576]{1,0:T(8,128)(2,1)}, bf16[64,576]{1,0:T(8,128)(2,1)}, bf16[64,576]{1,0:T(8,128)(2,1)}, bf16[64,576]{1,0:T(8,128)(2,1)}, bf16[64,576]{1,0:T(8,128)(2,1)}, /*index=5*/bf16[192,384]{1,0:T(8,128)(2,1)}) custom-call(s32[2]{0:T(128)} %pad_add_fusion.where_ref, s32[40]{0:T(128)} %occ_ref.3, s32[384]{0:T(512)} %vir_ref.3, ...), custom_call_target="tpu_custom_call" | custom-call | tf_op jit(solution)/shard_map/term/pallas_call | solution.py:206
  61.3 3.1 %collective-permute-start = (bf16[64,576]{1,0:T(8,128)(2,1)}, bf16[64,576]{1,0:T(8,128)(2,1)S(1)}, u32[]{:S(2)}, u32[]{:S(2)}) collective-permute-start(bf16[64,576]{1,0:T(8,128)(2,1)} %get-tuple-element.14), channel_id=1, source_target_pairs={{0,1},{1,2},{2,3},{3,0},{4,5},{5,6},{6,7},{7,4},{8,9},{9,10},{10,1... | collective-permute-start | bytes 221192 | tf_op jit(solution)/shard_map/ppermute | solution.py:259
  64.4 4.2 %collective-permute-start.1 = (bf16[64,576]{1,0:T(8,128)(2,1)}, bf16[64,576]{1,0:T(8,128)(2,1)S(1)}, u32[]{:S(2)}, u32[]{:S(2)}) collective-permute-start(bf16[64,576]{1,0:T(8,128)(2,1)} %get-tuple-element.15), channel_id=1, source_target_pairs={{0,2},{1,3},{2,0},{3,1},{4,6},{5,7},{6,4},{7,5},{8,10},{9,11},{10,... | collective-permute-start | bytes 221192 | tf_op jit(solution)/shard_map/ppermute | solution.py:259
  68.6 2.4 %collective-permute-start.2 = (bf16[64,576]{1,0:T(8,128)(2,1)}, bf16[64,576]{1,0:T(8,128)(2,1)S(1)}, u32[]{:S(2)}, u32[]{:S(2)}) collective-permute-start(bf16[64,576]{1,0:T(8,128)(2,1)} %get-tuple-element.16), channel_id=1, source_target_pairs={{0,3},{1,0},{2,1},{3,2},{4,7},{5,4},{6,5},{7,6},{8,11},{9,8},{10,9... | collective-permute-start | bytes 221192 | tf_op jit(solution)/shard_map/ppermute | solution.py:259
  71.0 0.0 copy-done.5
  71.0 0.6 reshape.7.energy_ref
  71.6 0.0 collective-permute-done.refs_2_
  71.6 0.0 copy-start.1
  71.6 3.8 %collective-permute-done.1.refs_3_ = bf16[64,576]{1,0:T(8,128)(2,1)S(1)} collective-permute-done((bf16[64,576]{1,0:T(8,128)(2,1)}, bf16[64,576]{1,0:T(8,128)(2,1)S(1)}, u32[]{:S(2)}, u32[]{:S(2)}) %collective-permute-start.1) | collective-permute-done | bytes 73760 | tf_op jit(solution)/shard_map/ppermute | solution.py:259
  75.4 0.0 copy-start.2
  75.4 0.0 collective-permute-done.2.refs_4_
  75.4 0.0 copy-start.3
  75.4 0.0 copy-done.1
  75.4 0.6 copy-done.2
  76.0 0.0 copy-done.3
  76.1 2.5 %finish.1 = f32[10,3,6,384]{3,2,1,0:T(8,128)} custom-call(s32[2]{0:T(128)} %pad_add_fusion.where_ref, s32[40]{0:T(128)} %occ_ref.3, s32[384]{0:T(512)} %vir_ref.3, f32[40]{0:T(128)} %occ_e_ref.1, f32[384]{0:T(512)} %vir_e_ref.1, s32[1,384]{1,0:T(1,128)} %reshape.6.label_ref, f32[1,384]{1,0:T(1,128)} %reshape.7.energy_ref, ...), custom_call_target="tpu_custom_call" | custom-call | tf_op jit(solution)/shard_map/finish/pallas_call | solution.py:241
Async XLA Ops:
  5.0 10.5 %copy-start.4 = (s32[384]{0:T(512)S(1)}, s32[384]{0:T(512)}, u32[]{:S(2)}) copy-start(s32[384]{0:T(512)} %vir_ref.3) | copy-start | bytes 4612
  5.0 38.6 %all-to-all-start = ((bf16[64,120,128]{2,1,0:T(8,128)(2,1)}), bf16[64,120,128]{2,1,0:T(8,128)(2,1)S(1)}, u32[]{:S(2)}, u32[]{:S(2)}) async-start(bf16[64,120,128]{2,1,0:T(8,128)(2,1)} %pack.1), calls=%async_computation | async-start | bytes 3932160 | tf_op jit(solution)/shard_map/all_to_all | solution.py:255
  43.6 1.3 %copy-start = (bf16[64,120,128]{2,1,0:T(8,128)(2,1)}, bf16[64,120,128]{2,1,0:T(8,128)(2,1)S(1)}, u32[]{:S(2)}) copy-start(bf16[64,120,128]{2,1,0:T(8,128)(2,1)S(1)} %all-to-all-done.got_ref) | copy-start | bytes 5898244
  44.9 26.1 %copy-start.5 = (f32[384]{0:T(512)S(1)}, f32[384]{0:T(512)}, u32[]{:S(2)}) copy-start(f32[384]{0:T(512)} %vir_e_ref.1) | copy-start | bytes 4612
  61.3 10.3 %collective-permute-start = (bf16[64,576]{1,0:T(8,128)(2,1)}, bf16[64,576]{1,0:T(8,128)(2,1)S(1)}, u32[]{:S(2)}, u32[]{:S(2)}) collective-permute-start(bf16[64,576]{1,0:T(8,128)(2,1)} %get-tuple-element.14), channel_id=1, source_target_pairs={{0,1},{1,2},{2,3},{3,0},{4,5},{5,6},{6,7},{7,4},{8,9},{9,10},{10,1... | collective-permute-start | bytes 221192 | tf_op jit(solution)/shard_map/ppermute | solution.py:259
  64.4 11.0 %collective-permute-start.1 = (bf16[64,576]{1,0:T(8,128)(2,1)}, bf16[64,576]{1,0:T(8,128)(2,1)S(1)}, u32[]{:S(2)}, u32[]{:S(2)}) collective-permute-start(bf16[64,576]{1,0:T(8,128)(2,1)} %get-tuple-element.15), channel_id=1, source_target_pairs={{0,2},{1,3},{2,0},{3,1},{4,6},{5,7},{6,4},{7,5},{8,10},{9,11},{10,... | collective-permute-start | bytes 221192 | tf_op jit(solution)/shard_map/ppermute | solution.py:259
  68.6 6.8 %collective-permute-start.2 = (bf16[64,576]{1,0:T(8,128)(2,1)}, bf16[64,576]{1,0:T(8,128)(2,1)S(1)}, u32[]{:S(2)}, u32[]{:S(2)}) collective-permute-start(bf16[64,576]{1,0:T(8,128)(2,1)} %get-tuple-element.16), channel_id=1, source_target_pairs={{0,3},{1,0},{2,1},{3,2},{4,7},{5,4},{6,5},{7,6},{8,11},{9,8},{10,9... | collective-permute-start | bytes 221192 | tf_op jit(solution)/shard_map/ppermute | solution.py:259
  71.6 3.8 %copy-start.1 = (bf16[64,576]{1,0:T(8,128)(2,1)}, bf16[64,576]{1,0:T(8,128)(2,1)S(1)}, u32[]{:S(2)}) copy-start(bf16[64,576]{1,0:T(8,128)(2,1)S(1)} %collective-permute-done.refs_2_) | copy-start | bytes 221188
  75.4 0.6 copy-start.2
  75.4 0.7 copy-start.3

commit v2 on v0

v2 whole, which is shorter than its diff:
```python
import jax
import jax.numpy as jnp
from jax import lax
from jax.experimental import pallas as pl
from jax.experimental.pallas import tpu as pltpu
from jax.sharding import PartitionSpec as P


OCC = 40
VIR = 384
OJW = 3
GRP = 64
CON = 4
PAIR = OCC * OCC // GRP
SEC = VIR // GRP
OWN = OCC // CON
SLOT = VIR // 2
WIDE = OJW * VIR
VMEM = pl.BlockSpec(memory_space=pltpu.VMEM)
SMEM = pl.BlockSpec(memory_space=pltpu.SMEM)
HBM = pl.BlockSpec(memory_space=pltpu.HBM)
MIB = 1024 * 1024
BF16, F32 = jnp.bfloat16, jnp.float32

COUPLES = 13
A_WIDTH, A_ROWS, A_BLOCK, A_STEPS = 64, 80, 512, 5
B_WIDTH, B_ROWS, B_BLOCK, B_STEPS = 32, 48, 640, 2


def nt_dot(x, y):
    return lax.dot_general(x, y, (((1,), (1,)), ((), ())), preferred_element_type=F32)


def picks():
    row = lax.broadcasted_iota(jnp.int32, (GRP * 8, 1), 0)
    dest, sub = row // 8, row % 8
    col = lax.broadcasted_iota(jnp.int32, (GRP * 8, VIR), 1)

    def pick(target):
        return jnp.where(col == target, 1.0, 0.0).astype(BF16)

    main = pick(jnp.where(sub < 6, dest * SEC + sub, -1))
    return main, [pick(jnp.where(sub >= 6, dest * SEC + 2 * j + sub - 6, -1)) for j in range(3)]


def store_tiles(out_ref, value, tile):
    out_ref[:, tile * 8 : tile * 8 + 8, :] = value.astype(BF16).reshape(GRP, 8, 128)


def pack_kernel(tiles, with_rest, pieces, first_c, width, x_hbm, out_ref, main_ref, rest_ref, sem):
    odd = lax.rem(lax.axis_index("grp"), 2)

    def fetch(lane_tile, dst, at):
        for n in range(pieces):
            pair = jnp.clip(pieces * lane_tile + n - odd, 0, PAIR - 1)
            pltpu.make_async_copy(
                x_hbm.at[pair, pl.ds(first_c, width)], dst.at[pl.ds(at + n * width, width)], sem
            ).start()

    for j in range(3):
        for n, lane_tile in enumerate(tiles[j]):
            fetch(lane_tile, main_ref.at[j], n * 128)
    for n, lane_tile in enumerate(with_rest):
        fetch(lane_tile, rest_ref, n * 128)
    main_pick, rest_picks = picks()
    for j in range(3):
        size = len(tiles[j]) * 128
        whole = main_ref.at[j, pl.ds(0, size)]
        pltpu.make_async_copy(whole, whole, sem).wait()
    pltpu.make_async_copy(rest_ref, rest_ref, sem).wait()
    for j in range(3):
        main = nt_dot(main_pick, main_ref[j, : len(tiles[j]) * 128])
        rest = nt_dot(rest_picks[j], rest_ref[...])
        for n in range(len(tiles[j])):
            value = main[:, n * 128 : n * 128 + 128]
            if n < len(with_rest):
                value = value + rest[:, n * 128 : n * 128 + 128]
            store_tiles(out_ref, value, 3 * n + j)


A_TILES, A_REST = ((0, 4, 8, 12), (1, 5, 9), (2, 6, 10)), (3, 7, 11)
B_TILES, B_REST = ((0, 4), (1, 5), (2, 6)), (3,)


def pack(x, rows, tiles, rest, pieces, first_c, width):
    def kernel(*refs):
        pack_kernel(tiles, rest, pieces, first_c, width, *refs)

    return pl.pallas_call(
        kernel,
        out_shape=jax.ShapeDtypeStruct((GRP, rows, 128), BF16),
        in_specs=[HBM],
        out_specs=VMEM,
        scratch_shapes=[
            pltpu.VMEM((3, len(tiles[0]) * 128, VIR), BF16),
            pltpu.VMEM((len(rest) * 128, VIR), BF16),
            pltpu.SemaphoreType.DMA,
        ],
        compiler_params=pltpu.CompilerParams(vmem_limit_bytes=12 * MIB),
        cost_estimate=pl.CostEstimate(flops=10**9, bytes_accessed=3 * 10**6, transcendentals=0),
    )(x)


def own_column(ref, first, dtype):
    row = lax.broadcasted_iota(jnp.int32, (8, 1), 0)
    column = jnp.zeros((8, 1), dtype)
    for a in range(SEC):
        column = jnp.where(row == a, ref[first + a], column)
    return column


def prepare_kernel(
    occ_ref, vir_ref, occ_e_ref, vir_e_ref, label_ref, energy_ref, w_hbm, wa_ref, wb_ref, fold_ref, scale_ref, sem
):
    def fetch(kq, carry):
        for n in range(4):
            for j in range(OJW):
                source = w_hbm.at[4 * kq + n, j]
                lanes = pl.ds(j * VIR, VIR)
                at_a = pl.multiple_of(kq * 256 + n * A_WIDTH, A_WIDTH)
                at_b = pl.multiple_of(kq * 128 + n * B_WIDTH, B_WIDTH)
                pltpu.make_async_copy(
                    source.at[pl.ds(0, A_WIDTH)], wa_ref.at[pl.ds(at_a, A_WIDTH), lanes], sem.at[0]
                ).start()
                pltpu.make_async_copy(
                    source.at[pl.ds(A_WIDTH, B_WIDTH)], wb_ref.at[pl.ds(at_b, B_WIDTH), lanes], sem.at[1]
                ).start()
        return carry

    lax.fori_loop(0, 10, fetch, 0)

    labels = label_ref[...]
    label_row = labels.astype(F32)
    label_col = jnp.transpose(jnp.broadcast_to(label_row, (8, VIR)))[:, :1]
    first = lax.broadcasted_iota(jnp.int32, (VIR, VIR), 0)
    second = lax.broadcasted_iota(jnp.int32, (VIR, VIR), 1)
    ahead = (label_col < label_row) | ((label_col == label_row) & (first < second))
    rank = jnp.sum(jnp.where(ahead, 1.0, 0.0), axis=0, keepdims=True)
    slot = jnp.where(rank >= SLOT, rank - SLOT, rank).astype(jnp.int32)
    fold_ref[...] = jnp.where(lax.broadcasted_iota(jnp.int32, (SLOT, VIR), 0) == slot, 1.0, 0.0).astype(BF16)

    own_i, own_a = lax.axis_index("con") * OWN, lax.axis_index("grp") * SEC
    label_ab = (own_column(vir_ref, own_a, jnp.int32) ^ labels)[:SEC]
    energy_ab = (own_column(vir_e_ref, own_a, F32) + energy_ref[...])[:SEC]
    for i in range(OWN):
        for j in range(OJW):
            keep = label_ab == (occ_ref[own_i + i] ^ occ_ref[j])
            denominator = occ_e_ref[own_i + i] + occ_e_ref[j] - energy_ab
            scale_ref[i, j] = jnp.where(keep, 1.0, 0.0) / denominator

    pltpu.make_async_copy(wa_ref, wa_ref, sem.at[0]).wait()
    pltpu.make_async_copy(wb_ref, wb_ref, sem.at[1]).wait()


def prepare(occ_irrep, vir_irrep, occ_energy, vir_energy, w):
    return pl.pallas_call(
        prepare_kernel,
        out_shape=[
            jax.ShapeDtypeStruct((OCC * A_WIDTH, WIDE), BF16),
            jax.ShapeDtypeStruct((OCC * B_WIDTH, WIDE), BF16),
            jax.ShapeDtypeStruct((SLOT, VIR), BF16),
            jax.ShapeDtypeStruct((OWN, OJW, SEC, VIR), F32),
        ],
        in_specs=[SMEM] * 4 + [VMEM] * 2 + [HBM],
        out_specs=[VMEM] * 4,
        scratch_shapes=[pltpu.SemaphoreType.DMA((2,))],
        compiler_params=pltpu.CompilerParams(vmem_limit_bytes=24 * MIB),
        cost_estimate=pl.CostEstimate(flops=10**8, bytes_accessed=20 * 10**6, transcendentals=0),
        name="prepare",
    )(
        occ_irrep,
        vir_irrep,
        occ_energy,
        vir_energy,
        vir_irrep.reshape(1, VIR),
        vir_energy.reshape(1, VIR),
        w,
    )


def lane_tiles(got_ref, s, rows, tiles, with_rest):
    got = got_ref[s].astype(F32).reshape(rows // 8, 8, 128)
    sub = lax.broadcasted_iota(jnp.int32, (8, 128), 0)
    found = {}
    for j in range(3):
        for n, lane_tile in enumerate(tiles[j]):
            found[lane_tile] = got[3 * n + j]
    for n, lane_tile in enumerate(with_rest):
        a, b, c = (pltpu.roll(got[3 * n + j], 2 + 2 * j, 0) for j in range(3))
        found[lane_tile] = jnp.where(sub < 2, a, jnp.where(sub < 4, b, c))
    return [found[t] for t in range(len(found))]


def store_couples(h, even, odd, half, couple_ref):
    lane = lax.broadcasted_iota(jnp.int32, (8, 128), 1)
    for u in range(COUPLES - 1):
        couple_ref[PAIR * h + u] = even[u]
        couple_ref[PAIR * h + COUPLES + u] = odd[u + 1]
    couple_ref[PAIR * h + COUPLES - 1] = jnp.where(lane < half, even[COUPLES - 1], odd[0])


def store_rows(lhs_ref, step, at, even, odd):
    half = OCC // 2 * 8
    lhs_ref[step, :half, pl.ds(at, 128)] = even.reshape(half, 128).astype(BF16)
    lhs_ref[step, half:, pl.ds(at, 128)] = odd.reshape(half, 128).astype(BF16)


def term_a_kernel(got_ref, w_ref, sum_ref, couple_ref, lhs_ref):
    def unpack(h, carry):
        even, odd = (lane_tiles(got_ref, 2 * h + n, A_ROWS, A_TILES, A_REST) for n in range(2))
        store_couples(h, even, odd, 64, couple_ref)
        return carry

    lax.fori_loop(0, GRP // 2, unpack, 0)

    lane = lax.broadcasted_iota(jnp.int32, (OCC // 2, 8, 128), 2)
    by_i = couple_ref.reshape(OCC, OCC // 2, 8, 128)
    by_parity = couple_ref.reshape(OCC // 2, 2, OCC // 2, 8, 128)

    def combine(kk, carry):
        first, second = by_i[2 * kk], by_i[2 * kk + 1]
        even = jnp.where(lane < 64, first, pltpu.roll(second, 64, 2))
        odd = jnp.where(lane < 64, pltpu.roll(first, 64, 2), second)
        even = 2.0 * by_parity[:, 0, kk] - even
        odd = 2.0 * by_parity[:, 1, kk] - odd
        store_rows(lhs_ref, kk // 4, pl.multiple_of(kk % 4 * 128, 128), even, odd)
        return carry

    lax.fori_loop(0, OCC // 2, combine, 0)
    multiply(lhs_ref, w_ref, sum_ref, A_BLOCK, A_STEPS, None)


def multiply(lhs_ref, w_ref, sum_ref, block, steps, before_ref):
    def body(b, carry):
        rows = pl.ds(pl.multiple_of(b * block, block), block)
        part = jnp.dot(lhs_ref[b], w_ref[rows, :], preferred_element_type=F32)

        @pl.when(b == 0)
        def _():
            sum_ref[...] = part if before_ref is None else before_ref[...] + part

        @pl.when(b > 0)
        def _():
            sum_ref[...] += part

        return carry

    lax.fori_loop(0, steps, body, 0)


def term_a(got, w):
    return pl.pallas_call(
        term_a_kernel,
        out_shape=jax.ShapeDtypeStruct((OCC * 8, WIDE), F32),
        in_specs=[VMEM] * 2,
        out_specs=VMEM,
        scratch_shapes=[
            pltpu.VMEM((OCC * OCC // 2, 8, 128), F32),
            pltpu.VMEM((A_STEPS, OCC * 8, A_BLOCK), BF16),
        ],
        compiler_params=pltpu.CompilerParams(vmem_limit_bytes=14 * MIB),
        cost_estimate=pl.CostEstimate(flops=2 * 10**9, bytes_accessed=20 * 10**6, transcendentals=0),
        name="term_a",
    )(got, w)


def term_b_kernel(occ_ref, vir_ref, label_ref, got_ref, w_ref, fold_ref, before_ref, *refs):
    outs, (couple_ref, lhs_ref, sum_ref) = refs[:5], refs[5:]
    me = lax.axis_index("con")

    def unpack(h, carry):
        both = []
        for n in range(2):
            tiles = lane_tiles(got_ref, 2 * h + n, B_ROWS, B_TILES, B_REST)
            rolled = [pltpu.roll(t, 64, 1) for t in tiles]
            both.append([(tiles, rolled)[u % 2][u // 2] for u in range(COUPLES)])
        store_couples(h, *both, 32, couple_ref)
        return carry

    lax.fori_loop(0, GRP // 2, unpack, 0)

    lane = lax.broadcasted_iota(jnp.int32, (OCC // 2, 8, 128), 2)
    by_i = couple_ref.reshape(OCC, OCC // 2, 8, 128)
    by_parity = couple_ref.reshape(OCC // 2, 2, OCC // 2, 8, 128)

    def quarters(parts):
        low = jnp.where(lane < 32, parts[0], parts[1])
        high = jnp.where(lane < 96, parts[2], parts[3])
        return jnp.where(lane < 64, low, high)

    def combine(kq, carry):
        crossed = [by_i[4 * kq + n] for n in range(4)]
        values = []
        for parity in range(2):
            parts = [
                crossed[n] if n == parity else pltpu.roll(crossed[n], (32 * (n - parity)) % 128, 2) for n in range(4)
            ]
            direct = jnp.where(
                lane < 64, by_parity[:, parity, 2 * kq], pltpu.roll(by_parity[:, parity, 2 * kq + 1], 64, 2)
            )
            values.append(2.0 * direct - quarters(parts))
        store_rows(lhs_ref, kq // 5, pl.multiple_of(kq % 5 * 128, 128), *values)
        return carry

    lax.fori_loop(0, OCC // 4, combine, 0)
    multiply(lhs_ref, w_ref, sum_ref, B_BLOCK, B_STEPS, before_ref)

    label_ab = own_column(vir_ref, lax.axis_index("grp") * SEC, jnp.int32) ^ label_ref[...]

    def mask(i, carry):
        rows = pl.ds(pl.multiple_of(i % 2 * (OCC // 2 * 8) + i // 2 * 8, 8), 8)
        for j in range(OJW):
            lanes = pl.ds(j * VIR, VIR)
            keep = label_ab == (occ_ref[i] ^ occ_ref[j])
            sum_ref[rows, lanes] = jnp.where(keep, sum_ref[rows, lanes], 0.0)
        return carry

    lax.fori_loop(0, OCC, mask, 0)

    half = OWN // 2 * 8
    row = lax.broadcasted_iota(jnp.int32, (64, OWN * 8), 0)
    col = lax.broadcasted_iota(jnp.int32, (64, OWN * 8), 1)
    i, a = row // SEC, row % SEC
    dense = jnp.where((row < OWN * SEC) & (col == i % 2 * half + i // 2 * 8 + a), 1.0, 0.0).astype(BF16)
    fold = fold_ref[...]
    for s in range(CON):
        owner = lax.rem(me + s, CON)
        evens = pl.ds(pl.multiple_of(owner * half, 8), half)
        odds = pl.ds(pl.multiple_of(OCC // 2 * 8 + owner * half, 8), half)
        for j in range(OJW):
            lanes = pl.ds(j * VIR, VIR)
            value = jnp.concatenate([sum_ref[evens, lanes], sum_ref[odds, lanes]], 0)
            high = value.astype(BF16)
            parts = [(outs[s], high)]
            if s == 0:
                parts.append((outs[4], (value - high.astype(F32)).astype(BF16)))
            for out, part in parts:
                part = jnp.dot(dense, part, preferred_element_type=F32).astype(BF16)
                out[:, j * SLOT : (j + 1) * SLOT] = nt_dot(part, fold).astype(BF16)


def term_b(occ_irrep, vir_irrep, got, w, fold, before):
    return pl.pallas_call(
        term_b_kernel,
        out_shape=[jax.ShapeDtypeStruct((64, OJW * SLOT), BF16)] * 5,
        in_specs=[SMEM, SMEM] + [VMEM] * 5,
        out_specs=[VMEM] * 5,
        scratch_shapes=[
            pltpu.VMEM((OCC * OCC // 2, 8, 128), F32),
            pltpu.VMEM((B_STEPS, OCC * 8, B_BLOCK), BF16),
            pltpu.VMEM((OCC * 8, WIDE), F32),
        ],
        compiler_params=pltpu.CompilerParams(vmem_limit_bytes=14 * MIB),
        cost_estimate=pl.CostEstimate(flops=10**9, bytes_accessed=10 * 10**6, transcendentals=0),
        name="term_b",
    )(occ_irrep, vir_irrep, vir_irrep.reshape(1, VIR), got, w, fold, before)


def finish_kernel(fold_ref, scale_ref, *refs):
    chunks, out_ref = refs[:5], refs[5]
    for j in range(OJW):
        total = jnp.zeros((64, VIR), F32)
        for chunk in chunks:
            total += jnp.dot(chunk[:, j * SLOT : (j + 1) * SLOT], fold_ref[...], preferred_element_type=F32)
        for i in range(OWN):
            out_ref[i, j] = total[i * SEC : (i + 1) * SEC] * scale_ref[i, j]


def finish(fold, scale, chunks):
    return pl.pallas_call(
        finish_kernel,
        out_shape=jax.ShapeDtypeStruct((OWN, OJW, SEC, VIR), F32),
        in_specs=[VMEM] * 7,
        out_specs=VMEM,
        compiler_params=pltpu.CompilerParams(vmem_limit_bytes=8 * MIB),
        name="finish",
    )(fold, scale, *chunks)


def shards(amplitudes, integrals, occ_energy, vir_energy, occ_irrep, vir_irrep):
    x = jnp.swapaxes(amplitudes, 1, 2)
    sent_a = pack(x, A_ROWS, A_TILES, A_REST, 2, 0, A_WIDTH)
    got_a = lax.all_to_all(sent_a, "grp", split_axis=0, concat_axis=0, tiled=True)
    sent_b = pack(x, B_ROWS, B_TILES, B_REST, 4, A_WIDTH, B_WIDTH)
    got_b = lax.all_to_all(sent_b, "grp", split_axis=0, concat_axis=0, tiled=True)
    wa, wb, fold, scale = prepare(
        occ_irrep, vir_irrep, occ_energy, vir_energy, jnp.swapaxes(integrals, 1, 2)
    )
    before = term_a(got_a, wa)
    chunks = term_b(occ_irrep, vir_irrep, got_b, wb, fold, before)
    arrived = [chunks[0], chunks[4]]
    for s in (2, 1, 3):
        arrived.append(lax.ppermute(chunks[s], "con", [(n, (n + s) % CON) for n in range(CON)]))
    return finish(fold, scale, arrived)


def solution(mesh):
    return jax.shard_map(
        shards,
        mesh=mesh,
        in_specs=(P("grp", None, "con"), P(None, "con", None, None), P(), P(), P(), P()),
        out_specs=P("con", None, "grp", None),
        check_vma=False,
    )
```

time: 133 us -> 87 us (0.65)
  blocking collectives: 51.1 us -> 0 us
  Pallas kernels: 0 us -> 28.6 us
  starting transfers between devices: 7.27 us -> 25.4 us
  local copies, waits for them, and re-layouts: 26.3 us -> 9.95 us
  waiting for transfers between devices: 33.5 us -> 22.4 us
  other arithmetic: 8.08 us -> 0 us
  matrix products: 5.73 us -> 0 us
    all_to_all x1 -> x0, blocking collectives: 51.1 us -> none  [shards(): lax.all_to_all(sectioned, 'grp', split_axis=1, concat_axis=0, tiled=True)]
    pallas_call x0 -> x6, Pallas kernels: none -> 28.6 us  [the longest x1 10.2 us: term_b(): pl.pallas_call(term_b_kernel, out_shape=[jax.ShapeDtypeStruct((64, OJW *...]
    all_to_all x1 -> x2, waiting for transfers between devices: 33.5 us -> 17.8 us  [the longest x1 16.3 us: shards(): lax.all_to_all(sent_a, 'grp', split_axis=0, concat_axis=0, tiled=True)]
    convert_element_type x2 -> x0, local copies, waits for them, and re-layouts: 9.96 us -> none  [combine_pairs(): crossed.astype(jnp.float32)]
    unnamed x8 -> x18, local copies, waits for them, and re-layouts: 0.03 us -> 9.94 us
    mul x2 -> x0, local copies, waits for them, and re-layouts: 9.91 us -> none  [combine_pairs(): 2.0 * direct.astype(jnp.float32) - crossed.astype(jnp.float32)]
    ppermute x0 -> x3, starting transfers between devices: none -> 9.67 us  [shards(): lax.ppermute(chunks[s], 'con', [(n, (n + s) % CON) for n in range(CON)])]
    all_to_all x1 -> x2, starting transfers between devices: 7.27 us -> 15.8 us  [the longest x1 10.3 us: shards(): lax.all_to_all(sent_a, 'grp', split_axis=0, concat_axis=0, tiled=True)]
  transfers between devices with their start and end apart: 1 -> 5, of which waited for: 1 -> 3; matrix products, arithmetic and copies ran while one was open for 0% -> 0% of each run, Pallas kernels for 0% -> 14%
where the time goes in v2:
time: 87 us; the launch traced here: 86.6 us
  Pallas kernels  28.6 us (33%)
  starting transfers between devices  25.4 us (29%)
  waiting for transfers between devices  22.4 us (26%)
  local copies, waits for them, and re-layouts  9.95 us (11%)
    all_to_all x1, waiting for transfers between devices, shards(): lax.all_to_all(sent_a, 'grp', split_axis=0, concat_axis=0, tiled=True)  16.3 us
    all_to_all x1, starting transfers between devices, shards(): lax.all_to_all(sent_a, 'grp', split_axis=0, concat_axis=0, tiled=True)  10.3 us
    pallas_call x1, Pallas kernels, term_b(): pl.pallas_call(term_b_kernel, out_shape=[jax.ShapeDtypeStruct((64, OJW *...  10.2 us
    unnamed x18, local copies, waits for them, and re-layouts  9.94 us
    ppermute x3, starting transfers between devices, shards(): lax.ppermute(chunks[s], 'con', [(n, (n + s) % CON) for n in range(CON)])  9.67 us
    pallas_call x2, Pallas kernels, pack(): pl.pallas_call(kernel, out_shape=jax.ShapeDtypeStruct((GRP, rows, 128), B...  8.19 us
    pallas_call x1, Pallas kernels, term_a(): pl.pallas_call(term_a_kernel, out_shape=jax.ShapeDtypeStruct((OCC * 8, WI...  6.19 us
    all_to_all x1, starting transfers between devices, shards(): lax.all_to_all(sent_b, 'grp', split_axis=0, concat_axis=0, tiled=True)  5.41 us
  transfers between devices with their start and end apart: 5, of which 3 were waited for; matrix products, arithmetic and copies ran while one was open for 0% of the time, Pallas kernels for 14%

profile of v2, /device:TPU:1, one launch (start us, length us, event | category | flops | bytes accessed | tf_op | source)
XLA Modules:
  0.0 86.6 jit_solution(9100906132015555193)
XLA Ops:
  0.0 0.0 copy-start.7
  0.0 1.5 %copy-done.7 = bf16[25,384,96]{1,2,0:T(8,128)(2,1)S(1)} copy-done((bf16[25,384,96]{1,2,0:T(8,128)(2,1)S(1)}, bf16[25,384,96]{1,2,0:T(8,128)(2,1)}, u32[]{:S(2)}) %copy-start.7) | copy-done | bytes 1843224
  1.5 4.9 %shard_map.65 = bf16[64,80,128]{2,1,0:T(8,128)(2,1)} custom-call(bf16[25,96,384]{2,1,0:T(8,128)(2,1)S(1)} %bitcast.3), custom_call_target="tpu_custom_call" | custom-call | flops 1000000000 | bytes 3000000 | tf_op jit(solution)/shard_map/pallas_call | solution.py:89
  6.4 10.3 %all-to-all-start.1 = ((bf16[64,80,128]{2,1,0:T(8,128)(2,1)}), bf16[64,80,128]{2,1,0:T(8,128)(2,1)S(1)}, u32[]{:S(2)}, u32[]{:S(2)}) async-start(bf16[64,80,128]{2,1,0:T(8,128)(2,1)} %shard_map.65), calls=%async_computation.1 | async-start | bytes 2621440 | tf_op jit(solution)/shard_map/all_to_all | solution.py:383
  16.8 0.0 copy-start.8
  16.8 1.5 %copy-done.8 = bf16[25,384,96]{1,2,0:T(8,128)(2,1)S(1)} copy-done((bf16[25,384,96]{1,2,0:T(8,128)(2,1)S(1)}, bf16[25,384,96]{1,2,0:T(8,128)(2,1)}, u32[]{:S(2)}) %copy-start.8) | copy-done | bytes 1843224
  18.3 0.0 copy-start.3
  18.3 0.0 copy-start.4
  18.3 0.0 copy-start.5
  18.3 0.0 copy-start.6
  18.3 3.3 %shard_map.64 = bf16[64,48,128]{2,1,0:T(8,128)(2,1)} custom-call(bf16[25,96,384]{2,1,0:T(8,128)(2,1)S(1)} %bitcast.4), custom_call_target="tpu_custom_call" | custom-call | flops 1000000000 | bytes 3000000 | tf_op jit(solution)/shard_map/pallas_call | solution.py:89
  21.6 16.3 %all-to-all-done.1.got_ref = bf16[64,80,128]{2,1,0:T(8,128)(2,1)S(1)} async-done(((bf16[64,80,128]{2,1,0:T(8,128)(2,1)}), bf16[64,80,128]{2,1,0:T(8,128)(2,1)S(1)}, u32[]{:S(2)}, u32[]{:S(2)}) %all-to-all-start.1) | async-done | bytes 1310752 | tf_op jit(solution)/shard_map/all_to_all | solution.py:383
  37.8 5.4 %all-to-all-start = ((bf16[64,48,128]{2,1,0:T(8,128)(2,1)}), bf16[64,48,128]{2,1,0:T(8,128)(2,1)}, u32[]{:S(2)}, u32[]{:S(2)}) async-start(bf16[64,48,128]{2,1,0:T(8,128)(2,1)} %shard_map.64), calls=%async_computation | async-start | bytes 1572864 | tf_op jit(solution)/shard_map/all_to_all | solution.py:385
  43.3 0.0 copy-done.3
  43.3 0.0 copy-done.4
  43.3 0.0 copy-done.5
  43.3 0.0 copy-done.6
  43.3 0.0 copy-start
  43.3 3.5 %copy-done = bf16[40,96,3,384]{3,1,2,0:T(8,128)(2,1)S(1)} copy-done((bf16[40,96,3,384]{3,1,2,0:T(8,128)(2,1)S(1)}, bf16[40,96,3,384]{3,1,2,0:T(8,128)(2,1)}, u32[]{:S(2)}) %copy-start) | copy-done | bytes 8847384
  46.8 2.6 %prepare.1 = (bf16[2560,1152]{1,0:T(8,128)(2,1)S(1)}, bf16[1280,1152]{1,0:T(8,128)(2,1)S(1)}, bf16[192,384]{1,0:T(8,128)(2,1)S(1)}, f32[10,3,6,384]{3,2,1,0:T(8,128)S(1)}) custom-call(s32[40]{0:T(128)S(1)} %copy-done.5, s32[384]{0:T(512)S(1)} %copy-done.3, f32[40]{0:T(128)S(1)} %copy-done.6, f32[384]{0:T(512)S(1)} %copy-done.4, ...), custom_call_target="tpu_custom_call" | custom-call | flops 100000000 | bytes 20000000 | tf_op jit(solution)/shard_map/prepare/pallas_call | solution.py:156
  49.5 0.0 copy-start.1
  49.5 1.6 %copy-done.1 = bf16[1280,1152]{1,0:T(8,128)(2,1)} copy-done((bf16[1280,1152]{1,0:T(8,128)(2,1)}, bf16[1280,1152]{1,0:T(8,128)(2,1)S(1)}, u32[]{:S(2)}) %copy-start.1) | copy-done | bytes 2949144
  51.1 6.2 %term_a.1.before_ref = f32[320,1152]{1,0:T(8,128)S(1)} custom-call(bf16[64,80,128]{2,1,0:T(8,128)(2,1)S(1)} %all-to-all-done.1.got_ref, bf16[2560,1152]{1,0:T(8,128)(2,1)S(1)} %get-tuple-element.17.w_ref), custom_call_target="tpu_custom_call" | custom-call | flops 2000000000 | bytes 20000000 | tf_op jit(solution)/shard_map/term_a/pallas_call | solution.py:252
  57.3 1.6 %all-to-all-done.got_ref = bf16[64,48,128]{2,1,0:T(8,128)(2,1)} async-done(((bf16[64,48,128]{2,1,0:T(8,128)(2,1)}), bf16[64,48,128]{2,1,0:T(8,128)(2,1)}, u32[]{:S(2)}, u32[]{:S(2)}) %all-to-all-start) | async-done | bytes 786464 | tf_op jit(solution)/shard_map/all_to_all | solution.py:385
  58.8 0.0 copy-start.2
  58.8 1.8 %copy-done.2 = bf16[1280,1152]{1,0:T(8,128)(2,1)S(1)} copy-done((bf16[1280,1152]{1,0:T(8,128)(2,1)S(1)}, bf16[1280,1152]{1,0:T(8,128)(2,1)}, u32[]{:S(2)}) %copy-start.2) | copy-done | bytes 2949144
  60.7 10.2 %term_b.1 = (bf16[64,576]{1,0:T(8,128)(2,1)S(1)}, bf16[64,576]{1,0:T(8,128)(2,1)S(1)}, bf16[64,576]{1,0:T(8,128)(2,1)S(1)}, bf16[64,576]{1,0:T(8,128)(2,1)S(1)}, bf16[64,576]{1,0:T(8,128)(2,1)S(1)}) custom-call(s32[40]{0:T(128)S(1)} %copy-done.5, s32[384]{0:T(512)S(1)} %copy-done.3, s32[1,384]{1,0:T(1,128)S(1)} %reshape.7.label_ref, ...), custom_call_target="tpu_custom_call" | custom-call | flops 1000000000 | bytes 10000000 | tf_op jit(solution)/shard_map/term_b/pallas_call | solution.py:343
  70.9 6.1 %collective-permute-start = (bf16[64,576]{1,0:T(8,128)(2,1)S(1)}, bf16[64,576]{1,0:T(8,128)(2,1)S(1)}, u32[]{:S(2)}, u32[]{:S(2)}) collective-permute-start(bf16[64,576]{1,0:T(8,128)(2,1)S(1)} %get-tuple-element.20), channel_id=1, source_target_pairs={{0,2},{1,3},{2,0},{3,1},{4,6},{5,7},{6,4},{7,5},{8,10},{9,11},{10,... | collective-permute-start | bytes 221192 | tf_op jit(solution)/shard_map/ppermute | solution.py:393
  77.0 1.2 %collective-permute-start.1 = (bf16[64,576]{1,0:T(8,128)(2,1)S(1)}, bf16[64,576]{1,0:T(8,128)(2,1)S(1)}, u32[]{:S(2)}, u32[]{:S(2)}) collective-permute-start(bf16[64,576]{1,0:T(8,128)(2,1)S(1)} %get-tuple-element.21), channel_id=1, source_target_pairs={{0,1},{1,2},{2,3},{3,0},{4,5},{5,6},{6,7},{7,4},{8,9},{9,10},{10,1... | collective-permute-start | bytes 221192 | tf_op jit(solution)/shard_map/ppermute | solution.py:393
  78.2 2.4 %collective-permute-start.2 = (bf16[64,576]{1,0:T(8,128)(2,1)S(1)}, bf16[64,576]{1,0:T(8,128)(2,1)S(1)}, u32[]{:S(2)}, u32[]{:S(2)}) collective-permute-start(bf16[64,576]{1,0:T(8,128)(2,1)S(1)} %get-tuple-element.22), channel_id=1, source_target_pairs={{0,3},{1,0},{2,1},{3,2},{4,7},{5,4},{6,5},{7,6},{8,11},{9,8},{10,9... | collective-permute-start | bytes 221192 | tf_op jit(solution)/shard_map/ppermute | solution.py:393
  80.6 0.0 collective-permute-done.refs_2_
  80.6 4.6 %collective-permute-done.1.refs_3_ = bf16[64,576]{1,0:T(8,128)(2,1)S(1)} collective-permute-done((bf16[64,576]{1,0:T(8,128)(2,1)S(1)}, bf16[64,576]{1,0:T(8,128)(2,1)S(1)}, u32[]{:S(2)}, u32[]{:S(2)}) %collective-permute-start.1) | collective-permute-done | bytes 73760 | tf_op jit(solution)/shard_map/ppermute | solution.py:393
  85.2 0.0 collective-permute-done.2.refs_4_
  85.2 1.4 %finish.1 = f32[10,3,6,384]{3,2,1,0:T(8,128)} custom-call(bf16[192,384]{1,0:T(8,128)(2,1)S(1)} %get-tuple-element.14.fold_ref, f32[10,3,6,384]{3,2,1,0:T(8,128)S(1)} %get-tuple-element.15.scale_ref, bf16[64,576]{1,0:T(8,128)(2,1)S(1)} %get-tuple-element.18.refs_0_, bf16[64,576]{1,0:T(8,128)(2,1)S(1)} %get-tuple-element.19.refs_1_, ...), custom_call_target="tpu_custom_call" | custom-call | tf_op jit(solution)/shard_map/finish/pallas_call | solution.py:370
  (2 shorter events, 0.0 us)
Async XLA Ops:
  0.0 1.5 %copy-start.7 = (bf16[25,384,96]{1,2,0:T(8,128)(2,1)S(1)}, bf16[25,384,96]{1,2,0:T(8,128)(2,1)}, u32[]{:S(2)}) copy-start(bf16[25,384,96]{1,2,0:T(8,128)(2,1)} %param.6) | copy-start | bytes 5529604
  6.4 31.4 %all-to-all-start.1 = ((bf16[64,80,128]{2,1,0:T(8,128)(2,1)}), bf16[64,80,128]{2,1,0:T(8,128)(2,1)S(1)}, u32[]{:S(2)}, u32[]{:S(2)}) async-start(bf16[64,80,128]{2,1,0:T(8,128)(2,1)} %shard_map.65), calls=%async_computation.1 | async-start | bytes 2621440 | tf_op jit(solution)/shard_map/all_to_all | solution.py:383
  16.8 1.5 %copy-start.8 = (bf16[25,384,96]{1,2,0:T(8,128)(2,1)S(1)}, bf16[25,384,96]{1,2,0:T(8,128)(2,1)}, u32[]{:S(2)}) copy-start(bf16[25,384,96]{1,2,0:T(8,128)(2,1)} %param.6) | copy-start | bytes 5529604
  18.3 25.0 %copy-start.3 = (s32[384]{0:T(512)S(1)}, s32[384]{0:T(512)}, u32[]{:S(2)}) copy-start(s32[384]{0:T(512)} %vir_ref.3) | copy-start | bytes 4612
  18.3 25.0 %copy-start.4 = (f32[384]{0:T(512)S(1)}, f32[384]{0:T(512)}, u32[]{:S(2)}) copy-start(f32[384]{0:T(512)} %vir_e_ref.1) | copy-start | bytes 4612
  18.3 25.0 %copy-start.5 = (s32[40]{0:T(128)S(1)}, s32[40]{0:T(128)}, u32[]{:S(2)}) copy-start(s32[40]{0:T(128)} %occ_ref.3) | copy-start | bytes 484
  18.3 25.0 %copy-start.6 = (f32[40]{0:T(128)S(1)}, f32[40]{0:T(128)}, u32[]{:S(2)}) copy-start(f32[40]{0:T(128)} %occ_e_ref.1) | copy-start | bytes 484
  37.8 21.0 %all-to-all-start = ((bf16[64,48,128]{2,1,0:T(8,128)(2,1)}), bf16[64,48,128]{2,1,0:T(8,128)(2,1)}, u32[]{:S(2)}, u32[]{:S(2)}) async-start(bf16[64,48,128]{2,1,0:T(8,128)(2,1)} %shard_map.64), calls=%async_computation | async-start | bytes 1572864 | tf_op jit(solution)/shard_map/all_to_all | solution.py:385
  43.3 3.5 %copy-start = (bf16[40,96,3,384]{3,1,2,0:T(8,128)(2,1)S(1)}, bf16[40,96,3,384]{3,1,2,0:T(8,128)(2,1)}, u32[]{:S(2)}) copy-start(bf16[40,96,3,384]{3,1,2,0:T(8,128)(2,1)} %param.7) | copy-start | bytes 26542084
  49.5 1.6 %copy-start.1 = (bf16[1280,1152]{1,0:T(8,128)(2,1)}, bf16[1280,1152]{1,0:T(8,128)(2,1)S(1)}, u32[]{:S(2)}) copy-start(bf16[1280,1152]{1,0:T(8,128)(2,1)S(1)} %get-tuple-element.16.w_ref) | copy-start | bytes 8847364
  58.8 1.8 %copy-start.2 = (bf16[1280,1152]{1,0:T(8,128)(2,1)S(1)}, bf16[1280,1152]{1,0:T(8,128)(2,1)}, u32[]{:S(2)}) copy-start(bf16[1280,1152]{1,0:T(8,128)(2,1)} %copy-done.1) | copy-start | bytes 8847364
  70.9 9.7 %collective-permute-start = (bf16[64,576]{1,0:T(8,128)(2,1)S(1)}, bf16[64,576]{1,0:T(8,128)(2,1)S(1)}, u32[]{:S(2)}, u32[]{:S(2)}) collective-permute-start(bf16[64,576]{1,0:T(8,128)(2,1)S(1)} %get-tuple-element.20), channel_id=1, source_target_pairs={{0,2},{1,3},{2,0},{3,1},{4,6},{5,7},{6,4},{7,5},{8,10},{9,11},{10,... | collective-permute-start | bytes 221192 | tf_op jit(solution)/shard_map/ppermute | solution.py:393
  77.0 8.2 %collective-permute-start.1 = (bf16[64,576]{1,0:T(8,128)(2,1)S(1)}, bf16[64,576]{1,0:T(8,128)(2,1)S(1)}, u32[]{:S(2)}, u32[]{:S(2)}) collective-permute-start(bf16[64,576]{1,0:T(8,128)(2,1)S(1)} %get-tuple-element.21), channel_id=1, source_target_pairs={{0,1},{1,2},{2,3},{3,0},{4,5},{5,6},{6,7},{7,4},{8,9},{9,10},{10,1... | collective-permute-start | bytes 221192 | tf_op jit(solution)/shard_map/ppermute | solution.py:393
  78.2 7.0 %collective-permute-start.2 = (bf16[64,576]{1,0:T(8,128)(2,1)S(1)}, bf16[64,576]{1,0:T(8,128)(2,1)S(1)}, u32[]{:S(2)}, u32[]{:S(2)}) collective-permute-start(bf16[64,576]{1,0:T(8,128)(2,1)S(1)} %get-tuple-element.22), channel_id=1, source_target_pairs={{0,3},{1,0},{2,1},{3,2},{4,7},{5,4},{6,5},{7,6},{8,11},{9,8},{10,9... | collective-permute-start | bytes 221192 | tf_op jit(solution)/shard_map/ppermute | solution.py:393

commit v3 on v0

v3 whole, which is shorter than its diff:
```python
import jax
import jax.numpy as jnp
from jax import lax
from jax.experimental import pallas as pl
from jax.experimental.pallas import tpu as pltpu
from jax.sharding import PartitionSpec as P


OCC = 40
VIR = 384
OJW = 3
GRP = 64
CON = 4
PAIR = OCC * OCC // GRP
SEC = VIR // GRP
CW = VIR // CON
OWN = OCC // CON
SLOT = VIR // 2
WIDE = OJW * VIR
VMEM = pl.BlockSpec(memory_space=pltpu.VMEM)
SMEM = pl.BlockSpec(memory_space=pltpu.SMEM)
HBM = pl.BlockSpec(memory_space=pltpu.HBM)
MIB = 1024 * 1024
TERM_LIMIT = 50 * MIB
BF16, F32 = jnp.bfloat16, jnp.float32

COUPLES = 13
TILES = 20
GROUPS = 5
ROWS = 120
A_WIDTH, B_WIDTH = 64, 32
BLOCK = 1280
STEPS = OCC * CW // BLOCK


def nt_dot(x, y):
    return lax.dot_general(x, y, (((1,), (1,)), ((), ())), preferred_element_type=F32)


def pack_kernel(x_hbm, out_hbm, main_ref, rest_ref, pick_ref, out_ref, sem, out_sem):
    odd = lax.rem(lax.axis_index("grp"), 2)
    for t in range(TILES):
        n, j = divmod(t, 4)
        dst = rest_ref if j == 3 else main_ref.at[j]
        for p in range(2 if t < COUPLES else 4):
            if t < COUPLES:
                pair, first_c, width = 2 * t + p, 0, A_WIDTH
            else:
                pair, first_c, width = 4 * (t - COUPLES) + p, A_WIDTH, B_WIDTH
            pltpu.make_async_copy(
                x_hbm.at[jnp.clip(pair - odd, 0, PAIR - 1), pl.ds(first_c, width)],
                dst.at[pl.ds(n * 128 + p * width, width)],
                sem,
            ).start()
    row = lax.broadcasted_iota(jnp.int32, (GRP * 4, 1), 0)
    dest, sub = row // 8, row % 8
    col = lax.broadcasted_iota(jnp.int32, (GRP * 4, 256), 1)

    def pick(target):
        return jnp.where(col == target, 1.0, 0.0).astype(BF16)

    for half in range(2):
        first = dest * SEC + 64 * half
        main = pick(jnp.where(sub < 6, first + sub, -1))
        for j in range(3):
            pick_ref[half, j, :, :256] = main
            pick_ref[half, j, :, 256:] = pick(jnp.where(sub >= 6, first + 2 * j + sub - 6, -1))
    pltpu.make_async_copy(main_ref, main_ref, sem).wait()
    pltpu.make_async_copy(rest_ref, rest_ref, sem).wait()
    for j in range(3):
        for half in range(2):
            lanes = slice(128 * half, 128 * half + 256)
            both = jnp.concatenate([main_ref[j, :, lanes], rest_ref[:, lanes]], 1)
            value = nt_dot(pick_ref[half, j], both).astype(BF16)
            for n in range(GROUPS):
                tile = value[:, n * 128 : n * 128 + 128].reshape(GRP // 2, 8, 128)
                out_ref[j, half * 32 : half * 32 + 32, n * 8 : n * 8 + 8, :] = tile
        pltpu.make_async_copy(out_ref.at[j], out_hbm.at[:, pl.ds(40 * j, 40)], out_sem.at[j]).start()
    for j in range(3):
        pltpu.make_async_copy(out_ref.at[j], out_hbm.at[:, pl.ds(40 * j, 40)], out_sem.at[j]).wait()


def pack(x):
    return pl.pallas_call(
        pack_kernel,
        out_shape=jax.ShapeDtypeStruct((GRP, ROWS, 128), BF16),
        in_specs=[HBM],
        out_specs=HBM,
        scratch_shapes=[
            pltpu.VMEM((3, GROUPS * 128, VIR), BF16),
            pltpu.VMEM((GROUPS * 128, VIR), BF16),
            pltpu.VMEM((2, 3, GRP * 4, 512), BF16),
            pltpu.VMEM((3, GRP, 40, 128), BF16),
            pltpu.SemaphoreType.DMA,
            pltpu.SemaphoreType.DMA((3,)),
        ],
        compiler_params=pltpu.CompilerParams(vmem_limit_bytes=62 * MIB),
        name="pack",
    )(x)


def own_column(ref, first, dtype):
    row = lax.broadcasted_iota(jnp.int32, (8, 1), 0)
    column = jnp.zeros((8, 1), dtype)
    for a in range(SEC):
        column = jnp.where(row == a, ref[first + a], column)
    return column


def prepare_kernel(
    occ_ref, vir_ref, occ_e_ref, vir_e_ref, label_ref, energy_ref, w_hbm, w_ref, fold_ref, scale_ref, sem
):
    def fetch(kq, carry):
        for n in range(4):
            for j in range(OJW):
                source = w_hbm.at[4 * kq + n, j]
                lanes = pl.ds(j * VIR, VIR)
                at_a = pl.multiple_of(kq * 256 + n * A_WIDTH, A_WIDTH)
                at_b = pl.multiple_of(OCC * A_WIDTH + kq * 128 + n * B_WIDTH, B_WIDTH)
                pltpu.make_async_copy(
                    source.at[pl.ds(0, A_WIDTH)], w_ref.at[pl.ds(at_a, A_WIDTH), lanes], sem
                ).start()
                pltpu.make_async_copy(
                    source.at[pl.ds(A_WIDTH, B_WIDTH)], w_ref.at[pl.ds(at_b, B_WIDTH), lanes], sem
                ).start()
        return carry

    lax.fori_loop(0, 10, fetch, 0)

    labels = label_ref[...]
    label_row = labels.astype(F32)
    label_col = jnp.transpose(jnp.broadcast_to(label_row, (8, VIR)))[:, :1]
    first = lax.broadcasted_iota(jnp.int32, (VIR, VIR), 0)
    second = lax.broadcasted_iota(jnp.int32, (VIR, VIR), 1)
    ahead = (label_col < label_row) | ((label_col == label_row) & (first < second))
    rank = jnp.sum(jnp.where(ahead, 1.0, 0.0), axis=0, keepdims=True)
    slot = jnp.where(rank >= SLOT, rank - SLOT, rank).astype(jnp.int32)
    fold_ref[...] = jnp.where(lax.broadcasted_iota(jnp.int32, (SLOT, VIR), 0) == slot, 1.0, 0.0).astype(BF16)

    own_i, own_a = lax.axis_index("con") * OWN, lax.axis_index("grp") * SEC
    label_ab = (own_column(vir_ref, own_a, jnp.int32) ^ labels)[:SEC]
    energy_ab = (own_column(vir_e_ref, own_a, F32) + energy_ref[...])[:SEC]
    for i in range(OWN):
        for j in range(OJW):
            keep = label_ab == (occ_ref[own_i + i] ^ occ_ref[j])
            denominator = occ_e_ref[own_i + i] + occ_e_ref[j] - energy_ab
            scale_ref[i, j] = jnp.where(keep, 1.0, 0.0) / denominator

    pltpu.make_async_copy(w_ref, w_ref, sem).wait()


def prepare(occ_irrep, vir_irrep, occ_energy, vir_energy, w):
    return pl.pallas_call(
        prepare_kernel,
        out_shape=[
            jax.ShapeDtypeStruct((OCC * CW, WIDE), BF16),
            jax.ShapeDtypeStruct((SLOT, VIR), BF16),
            jax.ShapeDtypeStruct((OWN, OJW, SEC, VIR), F32),
        ],
        in_specs=[SMEM] * 4 + [VMEM] * 2 + [HBM],
        out_specs=[VMEM] * 3,
        scratch_shapes=[pltpu.SemaphoreType.DMA],
        compiler_params=pltpu.CompilerParams(vmem_limit_bytes=24 * MIB),
        cost_estimate=pl.CostEstimate(flops=10**8, bytes_accessed=20 * 10**6, transcendentals=0),
        name="prepare",
    )(
        occ_irrep,
        vir_irrep,
        occ_energy,
        vir_energy,
        vir_irrep.reshape(1, VIR),
        vir_energy.reshape(1, VIR),
        w,
    )


def lane_tiles(got_ref, s):
    got = got_ref[s].astype(F32).reshape(ROWS // 8, 8, 128)
    sub = lax.broadcasted_iota(jnp.int32, (8, 128), 0)
    tiles = []
    for t in range(TILES):
        n, j = divmod(t, 4)
        if j < 3:
            tiles.append(got[GROUPS * j + n])
        else:
            a, b, c = (pltpu.roll(got[GROUPS * j + n], 2 + 2 * j, 0) for j in range(3))
            tiles.append(jnp.where(sub < 2, a, jnp.where(sub < 4, b, c)))
    return tiles


def store_couples(h, even, odd, half, couple_ref):
    lane = lax.broadcasted_iota(jnp.int32, (8, 128), 1)
    for u in range(COUPLES - 1):
        couple_ref[PAIR * h + u] = even[u]
        couple_ref[PAIR * h + COUPLES + u] = odd[u + 1]
    couple_ref[PAIR * h + COUPLES - 1] = jnp.where(lane < half, even[COUPLES - 1], odd[0])


def term_kernel(occ_ref, vir_ref, label_ref, got_ref, fold_ref, w_hbm, *refs):
    outs, own_ref, refs = refs[:3], refs[3], refs[4:]
    a_ref, b_ref, w_ref, sum_ref, masked_ref, sems = refs[:6]
    lhs_refs = refs[6:]
    me = lax.axis_index("con")
    half = OCC // 2 * 8

    def fetch(step):
        return pltpu.make_async_copy(w_hbm.at[pl.ds(step * BLOCK, BLOCK)], w_ref.at[step], sems.at[step])

    for step in range(STEPS):
        fetch(step).start()

    def unpack(h, carry):
        units_a, units_b = [], []
        for n in range(2):
            tiles = lane_tiles(got_ref, 2 * h + n)
            units_a.append(tiles[:COUPLES])
            units_b.append([
                tiles[COUPLES + u // 2] if u % 2 == 0 else pltpu.roll(tiles[COUPLES + u // 2], 64, 1)
                for u in range(COUPLES)
            ])
        store_couples(h, *units_a, 64, a_ref)
        store_couples(h, *units_b, 32, b_ref)
        return carry

    lax.fori_loop(0, GRP // 2, unpack, 0)

    lane = lax.broadcasted_iota(jnp.int32, (OCC // 2, 8, 128), 2)
    a_by_i, a_by_parity = a_ref.reshape(OCC, OCC // 2, 8, 128), a_ref.reshape(OCC // 2, 2, OCC // 2, 8, 128)
    b_by_i, b_by_parity = b_ref.reshape(OCC, OCC // 2, 8, 128), b_ref.reshape(OCC // 2, 2, OCC // 2, 8, 128)

    def combine_a(kk):
        first, second = a_by_i[2 * kk], a_by_i[2 * kk + 1]
        even = jnp.where(lane < 64, first, pltpu.roll(second, 64, 2))
        odd = jnp.where(lane < 64, pltpu.roll(first, 64, 2), second)
        return 2.0 * a_by_parity[:, 0, kk] - even, 2.0 * a_by_parity[:, 1, kk] - odd

    def combine_b(kq):
        crossed = [b_by_i[4 * kq + n] for n in range(4)]
        values = []
        for parity in range(2):
            part = [
                crossed[n] if n == parity else pltpu.roll(crossed[n], 32 * (n - parity) % 128, 2) for n in range(4)
            ]
            low, high = jnp.where(lane < 32, part[0], part[1]), jnp.where(lane < 96, part[2], part[3])
            direct = jnp.where(
                lane < 64, b_by_parity[:, parity, 2 * kq], pltpu.roll(b_by_parity[:, parity, 2 * kq + 1], 64, 2)
            )
            values.append(2.0 * direct - jnp.where(lane < 64, low, high))
        return values

    def combine(step):
        def body(n, carry):
            even, odd = combine_a(step * 10 + n) if step < 2 else combine_b(n)
            lanes = pl.ds(pl.multiple_of(n * 128, 128), 128)
            lhs_refs[step][:half, lanes] = even.reshape(half, 128).astype(BF16)
            lhs_refs[step][half:, lanes] = odd.reshape(half, 128).astype(BF16)
            return carry

        lax.fori_loop(0, 10, body, 0)

    for step in range(STEPS):
        combine(step)
        fetch(step).wait()
        part = jnp.dot(lhs_refs[step][...], w_ref[step], preferred_element_type=F32)
        sum_ref[...] = part if step == 0 else sum_ref[...] + part

    label_ab = own_column(vir_ref, lax.axis_index("grp") * SEC, jnp.int32) ^ label_ref[...]
    small = OWN // 2 * 8
    row = lax.broadcasted_iota(jnp.int32, (64, OWN * 8), 0)
    col = lax.broadcasted_iota(jnp.int32, (64, OWN * 8), 1)
    i, a = row // SEC, row % SEC
    dense = jnp.where((row < OWN * SEC) & (col == i % 2 * small + i // 2 * 8 + a), 1.0, 0.0).astype(BF16)
    for s in range(CON):
        owner = lax.rem(me + s, CON)
        for n in range(OWN):
            place = n % 2 * small + n // 2 * 8
            rows = pl.ds(pl.multiple_of(n % 2 * half + owner * small + n // 2 * 8, 8), 8)
            if s == 0:
                own_ref[place : place + 8, :] = sum_ref[rows, :]
                continue
            for j in range(OJW):
                keep = label_ab == (occ_ref[owner * OWN + n] ^ occ_ref[j])
                masked_ref[j * OWN * 8 + place : j * OWN * 8 + place + 8, :] = jnp.where(
                    keep, sum_ref[rows, j * VIR : (j + 1) * VIR], 0.0
                )
        if s > 0:
            folded = nt_dot(masked_ref[...].astype(BF16), fold_ref[...]).astype(BF16)
            for j in range(OJW):
                chunk = jnp.dot(dense, folded[j * OWN * 8 : (j + 1) * OWN * 8], preferred_element_type=F32)
                outs[s - 1][:, j * SLOT : (j + 1) * SLOT] = chunk.astype(BF16)


def term(occ_irrep, vir_irrep, got, fold, w):
    return pl.pallas_call(
        term_kernel,
        out_shape=[jax.ShapeDtypeStruct((64, OJW * SLOT), BF16)] * 3
        + [jax.ShapeDtypeStruct((OWN * 8, WIDE), F32)],
        in_specs=[SMEM, SMEM] + [VMEM] * 3 + [HBM],
        out_specs=[VMEM] * 4,
        scratch_shapes=[
            pltpu.VMEM((OCC * OCC // 2, 8, 128), F32),
            pltpu.VMEM((OCC * OCC // 2, 8, 128), F32),
            pltpu.VMEM((STEPS, BLOCK, WIDE), BF16),
            pltpu.VMEM((OCC * 8, WIDE), F32),
            pltpu.VMEM((OJW * OWN * 8, VIR), F32),
            pltpu.SemaphoreType.DMA((STEPS,)),
        ]
        + [pltpu.VMEM((OCC * 8, BLOCK), BF16)] * STEPS,
        compiler_params=pltpu.CompilerParams(vmem_limit_bytes=TERM_LIMIT),
        name="term",
    )(occ_irrep, vir_irrep, vir_irrep.reshape(1, VIR), got, fold, w)


def finish_kernel(fold_ref, scale_ref, own_ref, *refs):
    chunks, out_ref = refs[:3], refs[3]
    for j in range(OJW):
        lanes = slice(j * SLOT, (j + 1) * SLOT)
        stacked = jnp.concatenate([chunk[:, lanes] for chunk in chunks], 0)
        parts = jnp.dot(stacked, fold_ref[...], preferred_element_type=F32)
        total = parts[:64] + parts[64:128] + parts[128:]
        for i in range(OWN):
            place = i % 2 * (OWN // 2 * 8) + i // 2 * 8
            own = own_ref[place : place + SEC, j * VIR : (j + 1) * VIR]
            out_ref[i, j] = (own + total[i * SEC : (i + 1) * SEC]) * scale_ref[i, j]


def finish(fold, scale, own, chunks):
    return pl.pallas_call(
        finish_kernel,
        out_shape=jax.ShapeDtypeStruct((OWN, OJW, SEC, VIR), F32),
        in_specs=[VMEM] * 6,
        out_specs=VMEM,
        compiler_params=pltpu.CompilerParams(vmem_limit_bytes=8 * MIB),
        name="finish",
    )(fold, scale, own, *chunks)


def shards(amplitudes, integrals, occ_energy, vir_energy, occ_irrep, vir_irrep):
    sent = pack(jnp.swapaxes(amplitudes, 1, 2))
    got = lax.all_to_all(sent, "grp", split_axis=0, concat_axis=0, tiled=True)
    w, fold, scale = prepare(
        occ_irrep, vir_irrep, occ_energy, vir_energy, jnp.swapaxes(integrals, 1, 2)
    )
    *chunks, own = term(occ_irrep, vir_irrep, got, fold, w)
    arrived = [lax.ppermute(chunks[s - 1], "con", [(n, (n + s) % CON) for n in range(CON)]) for s in (2, 1, 3)]
    return finish(fold, scale, own, arrived)


def solution(mesh):
    return jax.shard_map(
        shards,
        mesh=mesh,
        in_specs=(P("grp", None, "con"), P(None, "con", None, None), P(), P(), P(), P()),
        out_specs=P("con", None, "grp", None),
        check_vma=False,
    )
```

time: 133 us -> 71 us (0.53)
  blocking collectives: 51.1 us -> 0 us
  Pallas kernels: 0 us -> 20.4 us
  local copies, waits for them, and re-layouts: 26.3 us -> 6.95 us
  starting transfers between devices: 7.27 us -> 20.2 us
  waiting for transfers between devices: 33.5 us -> 23.1 us
  other arithmetic: 8.08 us -> 0 us
  matrix products: 5.73 us -> 0 us
    all_to_all x1 -> x0, blocking collectives: 51.1 us -> none  [shards(): lax.all_to_all(sectioned, 'grp', split_axis=1, concat_axis=0, tiled=True)]
    pallas_call x0 -> x4, Pallas kernels: none -> 20.4 us  [the longest x1 12.8 us: term(): pl.pallas_call(term_kernel, out_shape=[jax.ShapeDtypeStruct((64, OJW * SL...]
    all_to_all x1, waiting for transfers between devices: 33.5 us -> 18.6 us  [shards(): got = lax.all_to_all(sent, 'grp', split_axis=0, concat_axis=0, tiled=True)]
    convert_element_type x2 -> x0, local copies, waits for them, and re-layouts: 9.96 us -> none  [combine_pairs(): crossed.astype(jnp.float32)]
    mul x2 -> x0, local copies, waits for them, and re-layouts: 9.91 us -> none  [combine_pairs(): 2.0 * direct.astype(jnp.float32) - crossed.astype(jnp.float32)]
    ppermute x0 -> x3, starting transfers between devices: none -> 9.67 us  [shards(): lax.ppermute(chunks[s - 1], 'con', [(n, (n + s) % CON) for n in range(CON)])]
    unnamed x8 -> x12, local copies, waits for them, and re-layouts: 0.03 us -> 6.94 us
    convert_element_type x2 -> x0, other arithmetic: 5.87 us -> none  [the longest x1 4.96 us: combine_pairs(): (2.0 * direct.astype(jnp.float32) - crossed.astype(jnp.float32)).astype(j...]
  transfers between devices with their start and end apart: 1 -> 4, of which waited for: 1 -> 2; matrix products, arithmetic and copies ran while one was open for 0% -> 0% of each run, Pallas kernels for 0% -> 4%
where the time goes in v3:
time: 71 us; the launch traced here: 70.7 us
  waiting for transfers between devices  23.1 us (33%)
  Pallas kernels  20.4 us (29%)
  starting transfers between devices  20.2 us (28%)
  local copies, waits for them, and re-layouts  6.95 us (10%)
    all_to_all x1, waiting for transfers between devices, shards(): got = lax.all_to_all(sent, 'grp', split_axis=0, concat_axis=0, tiled=True)  18.6 us
    pallas_call x1, Pallas kernels, term(): pl.pallas_call(term_kernel, out_shape=[jax.ShapeDtypeStruct((64, OJW * SL...  12.8 us
    all_to_all x1, starting transfers between devices, shards(): got = lax.all_to_all(sent, 'grp', split_axis=0, concat_axis=0, tiled=True)  10.5 us
    ppermute x3, starting transfers between devices, shards(): lax.ppermute(chunks[s - 1], 'con', [(n, (n + s) % CON) for n in range(CON)])  9.67 us
    unnamed x12, local copies, waits for them, and re-layouts  6.94 us
    ppermute x3, waiting for transfers between devices, shards(): lax.ppermute(chunks[s - 1], 'con', [(n, (n + s) % CON) for n in range(CON)])  4.52 us
    pallas_call x1, Pallas kernels, pack(): pl.pallas_call(pack_kernel, out_shape=jax.ShapeDtypeStruct((GRP, ROWS, 12...  3.93 us
    pallas_call x1, Pallas kernels, prepare(): pl.pallas_call(prepare_kernel, out_shape=[jax.ShapeDtypeStruct((OCC * CW,...  2.62 us
  transfers between devices with their start and end apart: 4, of which 2 were waited for; matrix products, arithmetic and copies ran while one was open for 0% of the time, Pallas kernels for 4%

profile of v3, /device:TPU:1, one launch (start us, length us, event | category | flops | bytes accessed | tf_op | source)
XLA Modules:
  0.0 70.7 jit_solution(14447775501056408716)
XLA Ops:
  0.0 3.9 %pack.1 = bf16[64,120,128]{2,1,0:T(8,128)(2,1)} custom-call(bf16[25,96,384]{2,1,0:T(8,128)(2,1)} %bitcast.3), custom_call_target="tpu_custom_call" | custom-call | tf_op jit(solution)/shard_map/pack/pallas_call | solution.py:84
  3.9 0.0 copy-start.2
  3.9 0.0 copy-start.3
  4.0 0.0 copy-start.4
  4.0 0.0 copy-start.5
  4.0 10.5 %all-to-all-start = ((bf16[64,120,128]{2,1,0:T(8,128)(2,1)}), bf16[64,120,128]{2,1,0:T(8,128)(2,1)S(1)}, u32[]{:S(2)}, u32[]{:S(2)}) async-start(bf16[64,120,128]{2,1,0:T(8,128)(2,1)} %pack.1), calls=%async_computation | async-start | bytes 3932160 | tf_op jit(solution)/shard_map/all_to_all | solution.py:340
  14.5 0.0 copy-done.2
  14.5 0.0 copy-done.3
  14.5 0.0 copy-done.4
  14.5 0.0 copy-done.5
  14.5 0.0 copy-start
  14.6 3.5 %copy-done = bf16[40,96,3,384]{3,1,2,0:T(8,128)(2,1)S(1)} copy-done((bf16[40,96,3,384]{3,1,2,0:T(8,128)(2,1)S(1)}, bf16[40,96,3,384]{3,1,2,0:T(8,128)(2,1)}, u32[]{:S(2)}) %copy-start) | copy-done | bytes 8847384
  18.1 2.6 %prepare.1 = (bf16[3840,1152]{1,0:T(8,128)(2,1)S(1)}, bf16[192,384]{1,0:T(8,128)(2,1)S(1)}, f32[10,3,6,384]{3,2,1,0:T(8,128)S(1)}) custom-call(s32[40]{0:T(128)S(1)} %copy-done.4, s32[384]{0:T(512)S(1)} %copy-done.2, f32[40]{0:T(128)S(1)} %copy-done.5, f32[384]{0:T(512)S(1)} %copy-done.3, s32[1,384]{1,0:T(1,128)S(1)} %reshape.7.label_ref, ...), custom_call_target="tpu_custom_call" | custom-call | flops 100000000 | bytes 20000000 | tf_op jit(solution)/shard_map/prepare/pallas_call | solution.py:153
  20.7 0.0 copy-start.1
  20.7 3.4 %copy-done.1 = bf16[3840,1152]{1,0:T(8,128)(2,1)} copy-done((bf16[3840,1152]{1,0:T(8,128)(2,1)}, bf16[3840,1152]{1,0:T(8,128)(2,1)S(1)}, u32[]{:S(2)}) %copy-start.1) | copy-done | bytes 8847384
  24.1 18.6 %all-to-all-done.got_ref = bf16[64,120,128]{2,1,0:T(8,128)(2,1)S(1)} async-done(((bf16[64,120,128]{2,1,0:T(8,128)(2,1)}), bf16[64,120,128]{2,1,0:T(8,128)(2,1)S(1)}, u32[]{:S(2)}, u32[]{:S(2)}) %all-to-all-start) | async-done | bytes 1966112 | tf_op jit(solution)/shard_map/all_to_all | solution.py:340
  42.7 12.8 %term.1 = (bf16[64,576]{1,0:T(8,128)(2,1)S(1)}, bf16[64,576]{1,0:T(8,128)(2,1)S(1)}, bf16[64,576]{1,0:T(8,128)(2,1)S(1)}, f32[80,1152]{1,0:T(8,128)S(1)}) custom-call(s32[40]{0:T(128)S(1)} %copy-done.4, s32[384]{0:T(512)S(1)} %copy-done.2, s32[1,384]{1,0:T(1,128)S(1)} %reshape.7.label_ref, bf16[64,120,128]{2,1,0:T(8,128)(2,1)S(1)} %all-to-all-done.got_ref, ...), custom_call_target="tpu_custom_call" | custom-call | tf_op jit(solution)/shard_map/term/pallas_call | solution.py:294
  55.4 6.1 %collective-permute-start = (bf16[64,576]{1,0:T(8,128)(2,1)S(1)}, bf16[64,576]{1,0:T(8,128)(2,1)S(1)}, u32[]{:S(2)}, u32[]{:S(2)}) collective-permute-start(bf16[64,576]{1,0:T(8,128)(2,1)S(1)} %get-tuple-element.16), channel_id=1, source_target_pairs={{0,2},{1,3},{2,0},{3,1},{4,6},{5,7},{6,4},{7,5},{8,10},{9,11},{10,... | collective-permute-start | bytes 221192 | tf_op jit(solution)/shard_map/ppermute | solution.py:345
  61.5 1.2 %collective-permute-start.1 = (bf16[64,576]{1,0:T(8,128)(2,1)S(1)}, bf16[64,576]{1,0:T(8,128)(2,1)S(1)}, u32[]{:S(2)}, u32[]{:S(2)}) collective-permute-start(bf16[64,576]{1,0:T(8,128)(2,1)S(1)} %get-tuple-element.17), channel_id=1, source_target_pairs={{0,1},{1,2},{2,3},{3,0},{4,5},{5,6},{6,7},{7,4},{8,9},{9,10},{10,1... | collective-permute-start | bytes 221192 | tf_op jit(solution)/shard_map/ppermute | solution.py:345
  62.7 2.4 %collective-permute-start.2 = (bf16[64,576]{1,0:T(8,128)(2,1)S(1)}, bf16[64,576]{1,0:T(8,128)(2,1)S(1)}, u32[]{:S(2)}, u32[]{:S(2)}) collective-permute-start(bf16[64,576]{1,0:T(8,128)(2,1)S(1)} %get-tuple-element.18), channel_id=1, source_target_pairs={{0,3},{1,0},{2,1},{3,2},{4,7},{5,4},{6,5},{7,6},{8,11},{9,8},{10,9... | collective-permute-start | bytes 221192 | tf_op jit(solution)/shard_map/ppermute | solution.py:345
  65.1 0.0 collective-permute-done.refs_0_
  65.1 4.5 %collective-permute-done.1.refs_1_ = bf16[64,576]{1,0:T(8,128)(2,1)S(1)} collective-permute-done((bf16[64,576]{1,0:T(8,128)(2,1)S(1)}, bf16[64,576]{1,0:T(8,128)(2,1)S(1)}, u32[]{:S(2)}, u32[]{:S(2)}) %collective-permute-start.1) | collective-permute-done | bytes 73760 | tf_op jit(solution)/shard_map/ppermute | solution.py:345
  69.6 0.0 collective-permute-done.2.refs_2_
  69.6 1.1 %finish.1 = f32[10,3,6,384]{3,2,1,0:T(8,128)} custom-call(bf16[192,384]{1,0:T(8,128)(2,1)S(1)} %get-tuple-element.12.fold_ref, f32[10,3,6,384]{3,2,1,0:T(8,128)S(1)} %get-tuple-element.13.scale_ref, f32[80,1152]{1,0:T(8,128)S(1)} %get-tuple-element.15.own_ref, bf16[64,576]{1,0:T(8,128)(2,1)S(1)} %collective-permute-done.refs_0_, ...), custom_call_target="tpu_custom_call" | custom-call | tf_op jit(solution)/shard_map/finish/pallas_call | solution.py:328
  (2 shorter events, 0.0 us)
Async XLA Ops:
  3.9 10.5 %copy-start.2 = (s32[384]{0:T(512)S(1)}, s32[384]{0:T(512)}, u32[]{:S(2)}) copy-start(s32[384]{0:T(512)} %vir_ref.3) | copy-start | bytes 4612
  3.9 10.6 %copy-start.3 = (f32[384]{0:T(512)S(1)}, f32[384]{0:T(512)}, u32[]{:S(2)}) copy-start(f32[384]{0:T(512)} %vir_e_ref.1) | copy-start | bytes 4612
  4.0 10.6 %copy-start.4 = (s32[40]{0:T(128)S(1)}, s32[40]{0:T(128)}, u32[]{:S(2)}) copy-start(s32[40]{0:T(128)} %occ_ref.3) | copy-start | bytes 484
  4.0 10.6 %copy-start.5 = (f32[40]{0:T(128)S(1)}, f32[40]{0:T(128)}, u32[]{:S(2)}) copy-start(f32[40]{0:T(128)} %occ_e_ref.1) | copy-start | bytes 484
  4.0 38.7 %all-to-all-start = ((bf16[64,120,128]{2,1,0:T(8,128)(2,1)}), bf16[64,120,128]{2,1,0:T(8,128)(2,1)S(1)}, u32[]{:S(2)}, u32[]{:S(2)}) async-start(bf16[64,120,128]{2,1,0:T(8,128)(2,1)} %pack.1), calls=%async_computation | async-start | bytes 3932160 | tf_op jit(solution)/shard_map/all_to_all | solution.py:340
  14.5 3.5 %copy-start = (bf16[40,96,3,384]{3,1,2,0:T(8,128)(2,1)S(1)}, bf16[40,96,3,384]{3,1,2,0:T(8,128)(2,1)}, u32[]{:S(2)}) copy-start(bf16[40,96,3,384]{3,1,2,0:T(8,128)(2,1)} %param.7) | copy-start | bytes 26542084
  20.7 3.4 %copy-start.1 = (bf16[3840,1152]{1,0:T(8,128)(2,1)}, bf16[3840,1152]{1,0:T(8,128)(2,1)S(1)}, u32[]{:S(2)}) copy-start(bf16[3840,1152]{1,0:T(8,128)(2,1)S(1)} %get-tuple-element.14.w_hbm) | copy-start | bytes 26542084
  55.4 9.7 %collective-permute-start = (bf16[64,576]{1,0:T(8,128)(2,1)S(1)}, bf16[64,576]{1,0:T(8,128)(2,1)S(1)}, u32[]{:S(2)}, u32[]{:S(2)}) collective-permute-start(bf16[64,576]{1,0:T(8,128)(2,1)S(1)} %get-tuple-element.16), channel_id=1, source_target_pairs={{0,2},{1,3},{2,0},{3,1},{4,6},{5,7},{6,4},{7,5},{8,10},{9,11},{10,... | collective-permute-start | bytes 221192 | tf_op jit(solution)/shard_map/ppermute | solution.py:345
  61.5 8.1 %collective-permute-start.1 = (bf16[64,576]{1,0:T(8,128)(2,1)S(1)}, bf16[64,576]{1,0:T(8,128)(2,1)S(1)}, u32[]{:S(2)}, u32[]{:S(2)}) collective-permute-start(bf16[64,576]{1,0:T(8,128)(2,1)S(1)} %get-tuple-element.17), channel_id=1, source_target_pairs={{0,1},{1,2},{2,3},{3,0},{4,5},{5,6},{6,7},{7,4},{8,9},{9,10},{10,1... | collective-permute-start | bytes 221192 | tf_op jit(solution)/shard_map/ppermute | solution.py:345
  62.7 6.9 %collective-permute-start.2 = (bf16[64,576]{1,0:T(8,128)(2,1)S(1)}, bf16[64,576]{1,0:T(8,128)(2,1)S(1)}, u32[]{:S(2)}, u32[]{:S(2)}) collective-permute-start(bf16[64,576]{1,0:T(8,128)(2,1)S(1)} %get-tuple-element.18), channel_id=1, source_target_pairs={{0,3},{1,0},{2,1},{3,2},{4,7},{5,4},{6,5},{7,6},{8,11},{9,8},{10,9... | collective-permute-start | bytes 221192 | tf_op jit(solution)/shard_map/ppermute | solution.py:345

commit v4 on v3

--- a/solution.py
+++ b/solution.py
@@ -38,17 +38,18 @@
 
 
 def pack_kernel(x_hbm, out_hbm, main_ref, rest_ref, pick_ref, out_ref, sem, out_sem):
-    odd = lax.rem(lax.axis_index("grp"), 2)
+    me = lax.axis_index("grp")
+    odd, phase = lax.rem(me, 2), lax.rem(me, 4)
     for t in range(TILES):
         n, j = divmod(t, 4)
         dst = rest_ref if j == 3 else main_ref.at[j]
         for p in range(2 if t < COUPLES else 4):
             if t < COUPLES:
-                pair, first_c, width = 2 * t + p, 0, A_WIDTH
+                pair, first_c, width = 2 * t + p - odd, 0, A_WIDTH
             else:
-                pair, first_c, width = 4 * (t - COUPLES) + p, A_WIDTH, B_WIDTH
+                pair, first_c, width = 4 * (t - COUPLES) + p - phase, A_WIDTH, B_WIDTH
             pltpu.make_async_copy(
-                x_hbm.at[jnp.clip(pair - odd, 0, PAIR - 1), pl.ds(first_c, width)],
+                x_hbm.at[jnp.clip(pair, 0, PAIR - 1), pl.ds(first_c, width)],
                 dst.at[pl.ds(n * 128 + p * width, width)],
                 sem,
             ).start()
@@ -188,20 +189,11 @@
     return tiles
 
 
-def store_couples(h, even, odd, half, couple_ref):
-    lane = lax.broadcasted_iota(jnp.int32, (8, 128), 1)
-    for u in range(COUPLES - 1):
-        couple_ref[PAIR * h + u] = even[u]
-        couple_ref[PAIR * h + COUPLES + u] = odd[u + 1]
-    couple_ref[PAIR * h + COUPLES - 1] = jnp.where(lane < half, even[COUPLES - 1], odd[0])
-
-
 def term_kernel(occ_ref, vir_ref, label_ref, got_ref, fold_ref, w_hbm, *refs):
     outs, own_ref, refs = refs[:3], refs[3], refs[4:]
     a_ref, b_ref, w_ref, sum_ref, masked_ref, sems = refs[:6]
     lhs_refs = refs[6:]
     me = lax.axis_index("con")
-    half = OCC // 2 * 8
 
     def fetch(step):
         return pltpu.make_async_copy(w_hbm.at[pl.ds(step * BLOCK, BLOCK)], w_ref.at[step], sems.at[step])
@@ -209,80 +201,90 @@
     for step in range(STEPS):
         fetch(step).start()
 
+    lane2 = lax.broadcasted_iota(jnp.int32, (8, 128), 1)
+
     def unpack(h, carry):
-        units_a, units_b = [], []
+        last_a = last_b = None
+        for n in range(4):
+            tiles = lane_tiles(got_ref, 4 * h + n)
+            units_a, units_b = tiles[:COUPLES], tiles[COUPLES:]
+            if n % 2:
+                units_a[0] = jnp.where(lane2 < 64, last_a, units_a[0])
+            if n > 0:
+                units_b[0] = jnp.where(lane2 < 32 * n, last_b, units_b[0])
+            last_a, last_b = units_a[-1], units_b[-1]
+            for u in range(COUPLES if n % 2 else COUPLES - 1):
+                a_ref[50 * h + 25 * n // 2 + u] = units_a[u]
+            for u in range(7 if n == 3 else 6):
+                b_ref[25 * h + 6 * n + u] = units_b[u]
+        return carry
+
+    lax.fori_loop(0, GRP // 4, unpack, 0)
+
+    ten = OCC // 4
+    lane = lax.broadcasted_iota(jnp.int32, (OCC // 2, 8, 128), 2)
+    lane_b = lax.broadcasted_iota(jnp.int32, (ten, 8, 128), 2)
+    a_by_i, a_by_m = a_ref.reshape(OCC, OCC // 2, 8, 128), a_ref.reshape(ten, 4, OCC // 2, 8, 128)
+    b_by_i, b_by_m = b_ref.reshape(OCC, ten, 8, 128), b_ref.reshape(ten, 4, ten, 8, 128)
+
+    def crossed_a(kk):
+        first, second = a_by_i[2 * kk], a_by_i[2 * kk + 1]
+        even = jnp.where(lane < 64, first, pltpu.roll(second, 64, 2)).reshape(ten, 2, 8, 128)
+        odd = jnp.where(lane < 64, pltpu.roll(first, 64, 2), second).reshape(ten, 2, 8, 128)
+        return even[:, 0], odd[:, 0], even[:, 1], odd[:, 1]
+
+    def crossed_b(kq):
+        c = [b_by_i[4 * kq + n] for n in range(4)]
+        low, upper = lane_b < 64, lane_b % 64 >= 32
+        wide = []
         for n in range(2):
-            tiles = lane_tiles(got_ref, 2 * h + n)
-            units_a.append(tiles[:COUPLES])
-            units_b.append([
-                tiles[COUPLES + u // 2] if u % 2 == 0 else pltpu.roll(tiles[COUPLES + u // 2], 64, 1)
-                for u in range(COUPLES)
-            ])
-        store_couples(h, *units_a, 64, a_ref)
-        store_couples(h, *units_b, 32, b_ref)
+            wide.append(jnp.where(low, c[n], pltpu.roll(c[n + 2], 64, 2)))
+        for n in range(2):
+            wide.append(jnp.where(low, pltpu.roll(c[n], 64, 2), c[n + 2]))
+        found = []
+        for m in (0, 2):
+            found.append(jnp.where(upper, pltpu.roll(wide[m + 1], 32, 2), wide[m]))
+            found.append(jnp.where(upper, wide[m + 1], pltpu.roll(wide[m], 96, 2)))
+        return found
+
+    def combine(step, n, lanes):
+        if step < 2:
+            by_m, k, crossed = a_by_m, step * 10 + n, crossed_a(step * 10 + n)
+        else:
+            by_m, k, crossed = b_by_m, n, crossed_b(n)
+        for m in range(4):
+            value = 2.0 * by_m[:, m, k] - crossed[m]
+            lhs_refs[step][m * ten * 8 : (m + 1) * ten * 8, lanes] = value.reshape(ten * 8, 128).astype(BF16)
+
+    def combine_first(n, carry):
+        combine(0, n, pl.ds(pl.multiple_of(n * 128, 128), 128))
         return carry
 
-    lax.fori_loop(0, GRP // 2, unpack, 0)
-
-    lane = lax.broadcasted_iota(jnp.int32, (OCC // 2, 8, 128), 2)
-    a_by_i, a_by_parity = a_ref.reshape(OCC, OCC // 2, 8, 128), a_ref.reshape(OCC // 2, 2, OCC // 2, 8, 128)
-    b_by_i, b_by_parity = b_ref.reshape(OCC, OCC // 2, 8, 128), b_ref.reshape(OCC // 2, 2, OCC // 2, 8, 128)
-
-    def combine_a(kk):
-        first, second = a_by_i[2 * kk], a_by_i[2 * kk + 1]
-        even = jnp.where(lane < 64, first, pltpu.roll(second, 64, 2))
-        odd = jnp.where(lane < 64, pltpu.roll(first, 64, 2), second)
-        return 2.0 * a_by_parity[:, 0, kk] - even, 2.0 * a_by_parity[:, 1, kk] - odd
-
-    def combine_b(kq):
-        crossed = [b_by_i[4 * kq + n] for n in range(4)]
-        values = []
-        for parity in range(2):
-            part = [
-                crossed[n] if n == parity else pltpu.roll(crossed[n], 32 * (n - parity) % 128, 2) for n in range(4)
-            ]
-            low, high = jnp.where(lane < 32, part[0], part[1]), jnp.where(lane < 96, part[2], part[3])
-            direct = jnp.where(
-                lane < 64, b_by_parity[:, parity, 2 * kq], pltpu.roll(b_by_parity[:, parity, 2 * kq + 1], 64, 2)
-            )
-            values.append(2.0 * direct - jnp.where(lane < 64, low, high))
-        return values
-
-    def combine(step):
-        def body(n, carry):
-            even, odd = combine_a(step * 10 + n) if step < 2 else combine_b(n)
-            lanes = pl.ds(pl.multiple_of(n * 128, 128), 128)
-            lhs_refs[step][:half, lanes] = even.reshape(half, 128).astype(BF16)
-            lhs_refs[step][half:, lanes] = odd.reshape(half, 128).astype(BF16)
-            return carry
-
-        lax.fori_loop(0, 10, body, 0)
-
+    lax.fori_loop(0, 10, combine_first, 0)
     for step in range(STEPS):
-        combine(step)
         fetch(step).wait()
+        if step + 1 < STEPS:
+            for n in range(10):
+                combine(step + 1, n, slice(n * 128, n * 128 + 128))
         part = jnp.dot(lhs_refs[step][...], w_ref[step], preferred_element_type=F32)
         sum_ref[...] = part if step == 0 else sum_ref[...] + part
 
     label_ab = own_column(vir_ref, lax.axis_index("grp") * SEC, jnp.int32) ^ label_ref[...]
-    small = OWN // 2 * 8
     row = lax.broadcasted_iota(jnp.int32, (64, OWN * 8), 0)
     col = lax.broadcasted_iota(jnp.int32, (64, OWN * 8), 1)
-    i, a = row // SEC, row % SEC
-    dense = jnp.where((row < OWN * SEC) & (col == i % 2 * small + i // 2 * 8 + a), 1.0, 0.0).astype(BF16)
+    dense = jnp.where((row < OWN * SEC) & (col == row // SEC * 8 + row % SEC), 1.0, 0.0).astype(BF16)
     for s in range(CON):
         owner = lax.rem(me + s, CON)
         for n in range(OWN):
-            place = n % 2 * small + n // 2 * 8
-            rows = pl.ds(pl.multiple_of(n % 2 * half + owner * small + n // 2 * 8, 8), 8)
+            i = owner * OWN + n
+            rows = pl.ds(pl.multiple_of((lax.rem(i, 4) * ten + lax.div(i, 4)) * 8, 8), 8)
             if s == 0:
-                own_ref[place : place + 8, :] = sum_ref[rows, :]
+                own_ref[n * 8 : n * 8 + 8, :] = sum_ref[rows, :]
                 continue
             for j in range(OJW):
-                keep = label_ab == (occ_ref[owner * OWN + n] ^ occ_ref[j])
-                masked_ref[j * OWN * 8 + place : j * OWN * 8 + place + 8, :] = jnp.where(
-                    keep, sum_ref[rows, j * VIR : (j + 1) * VIR], 0.0
-                )
+                keep = label_ab == (occ_ref[i] ^ occ_ref[j])
+                at = (j * OWN + n) * 8
+                masked_ref[at : at + 8, :] = jnp.where(keep, sum_ref[rows, j * VIR : (j + 1) * VIR], 0.0)
         if s > 0:
             folded = nt_dot(masked_ref[...].astype(BF16), fold_ref[...]).astype(BF16)
             for j in range(OJW):
@@ -299,7 +301,7 @@
         out_specs=[VMEM] * 4,
         scratch_shapes=[
             pltpu.VMEM((OCC * OCC // 2, 8, 128), F32),
-            pltpu.VMEM((OCC * OCC // 2, 8, 128), F32),
+            pltpu.VMEM((OCC * OCC // 4, 8, 128), F32),
             pltpu.VMEM((STEPS, BLOCK, WIDE), BF16),
             pltpu.VMEM((OCC * 8, WIDE), F32),
             pltpu.VMEM((OJW * OWN * 8, VIR), F32),
@@ -319,8 +321,7 @@
         parts = jnp.dot(stacked, fold_ref[...], preferred_element_type=F32)
         total = parts[:64] + parts[64:128] + parts[128:]
         for i in range(OWN):
-            place = i % 2 * (OWN // 2 * 8) + i // 2 * 8
-            own = own_ref[place : place + SEC, j * VIR : (j + 1) * VIR]
+            own = own_ref[i * 8 : i * 8 + SEC, j * VIR : (j + 1) * VIR]
             out_ref[i, j] = (own + total[i * SEC : (i + 1) * SEC]) * scale_ref[i, j]
 
 

time: 71 us -> 65.6 us (0.924)
  Pallas kernels: 20.4 us -> 14.9 us
    pallas_call x1, Pallas kernels: 12.8 us -> 7.3 us  [term(): pl.pallas_call(term_kernel, out_shape=[jax.ShapeDtypeStruct((64, OJW * SL...]
where the time goes in v4:
time: 65.6 us; the launch traced here: 65.2 us
  waiting for transfers between devices  23.1 us (35%)
  starting transfers between devices  20.2 us (31%)
  Pallas kernels  14.9 us (23%)
  local copies, waits for them, and re-layouts  6.95 us (11%)
    all_to_all x1, waiting for transfers between devices, shards(): got = lax.all_to_all(sent, 'grp', split_axis=0, concat_axis=0, tiled=True)  18.6 us
    all_to_all x1, starting transfers between devices, shards(): got = lax.all_to_all(sent, 'grp', split_axis=0, concat_axis=0, tiled=True)  10.5 us
    ppermute x3, starting transfers between devices, shards(): lax.ppermute(chunks[s - 1], 'con', [(n, (n + s) % CON) for n in range(CON)])  9.67 us
    pallas_call x1, Pallas kernels, term(): pl.pallas_call(term_kernel, out_shape=[jax.ShapeDtypeStruct((64, OJW * SL...  7.3 us
    unnamed x12, local copies, waits for them, and re-layouts  6.94 us
    ppermute x3, waiting for transfers between devices, shards(): lax.ppermute(chunks[s - 1], 'con', [(n, (n + s) % CON) for n in range(CON)])  4.52 us
    pallas_call x1, Pallas kernels, pack(): pl.pallas_call(pack_kernel, out_shape=jax.ShapeDtypeStruct((GRP, ROWS, 12...  3.93 us
    pallas_call x1, Pallas kernels, prepare(): pl.pallas_call(prepare_kernel, out_shape=[jax.ShapeDtypeStruct((OCC * CW,...  2.62 us
  transfers between devices with their start and end apart: 4, of which 2 were waited for; matrix products, arithmetic and copies ran while one was open for 0% of the time, Pallas kernels for 4%

profile of v4, /device:TPU:1, one launch (start us, length us, event | category | flops | bytes accessed | tf_op | source)
XLA Modules:
  0.0 65.2 jit_solution(4213809309229222739)
XLA Ops:
  0.0 3.9 %pack.1 = bf16[64,120,128]{2,1,0:T(8,128)(2,1)} custom-call(bf16[25,96,384]{2,1,0:T(8,128)(2,1)} %bitcast.3), custom_call_target="tpu_custom_call" | custom-call | tf_op jit(solution)/shard_map/pack/pallas_call | solution.py:85
  3.9 0.0 copy-start.2
  3.9 0.0 copy-start.3
  4.0 0.0 copy-start.4
  4.0 0.0 copy-start.5
  4.0 10.5 %all-to-all-start = ((bf16[64,120,128]{2,1,0:T(8,128)(2,1)}), bf16[64,120,128]{2,1,0:T(8,128)(2,1)S(1)}, u32[]{:S(2)}, u32[]{:S(2)}) async-start(bf16[64,120,128]{2,1,0:T(8,128)(2,1)} %pack.1), calls=%async_computation | async-start | bytes 3932160 | tf_op jit(solution)/shard_map/all_to_all | solution.py:341
  14.5 0.0 copy-done.2
  14.5 0.0 copy-done.3
  14.5 0.0 copy-done.4
  14.5 0.0 copy-done.5
  14.5 0.0 copy-start
  14.6 3.5 %copy-done = bf16[40,96,3,384]{3,1,2,0:T(8,128)(2,1)S(1)} copy-done((bf16[40,96,3,384]{3,1,2,0:T(8,128)(2,1)S(1)}, bf16[40,96,3,384]{3,1,2,0:T(8,128)(2,1)}, u32[]{:S(2)}) %copy-start) | copy-done | bytes 8847384
  18.1 2.6 %prepare.1 = (bf16[3840,1152]{1,0:T(8,128)(2,1)S(1)}, bf16[192,384]{1,0:T(8,128)(2,1)S(1)}, f32[10,3,6,384]{3,2,1,0:T(8,128)S(1)}) custom-call(s32[40]{0:T(128)S(1)} %copy-done.4, s32[384]{0:T(512)S(1)} %copy-done.2, f32[40]{0:T(128)S(1)} %copy-done.5, f32[384]{0:T(512)S(1)} %copy-done.3, s32[1,384]{1,0:T(1,128)S(1)} %reshape.7.label_ref, ...), custom_call_target="tpu_custom_call" | custom-call | flops 100000000 | bytes 20000000 | tf_op jit(solution)/shard_map/prepare/pallas_call | solution.py:154
  20.7 0.0 copy-start.1
  20.7 3.4 %copy-done.1 = bf16[3840,1152]{1,0:T(8,128)(2,1)} copy-done((bf16[3840,1152]{1,0:T(8,128)(2,1)}, bf16[3840,1152]{1,0:T(8,128)(2,1)S(1)}, u32[]{:S(2)}) %copy-start.1) | copy-done | bytes 8847384
  24.1 18.6 %all-to-all-done.got_ref = bf16[64,120,128]{2,1,0:T(8,128)(2,1)S(1)} async-done(((bf16[64,120,128]{2,1,0:T(8,128)(2,1)}), bf16[64,120,128]{2,1,0:T(8,128)(2,1)S(1)}, u32[]{:S(2)}, u32[]{:S(2)}) %all-to-all-start) | async-done | bytes 1966112 | tf_op jit(solution)/shard_map/all_to_all | solution.py:341
  42.7 7.3 %term.1 = (bf16[64,576]{1,0:T(8,128)(2,1)S(1)}, bf16[64,576]{1,0:T(8,128)(2,1)S(1)}, bf16[64,576]{1,0:T(8,128)(2,1)S(1)}, f32[80,1152]{1,0:T(8,128)S(1)}) custom-call(s32[40]{0:T(128)S(1)} %copy-done.4, s32[384]{0:T(512)S(1)} %copy-done.2, s32[1,384]{1,0:T(1,128)S(1)} %reshape.7.label_ref, bf16[64,120,128]{2,1,0:T(8,128)(2,1)S(1)} %all-to-all-done.got_ref, ...), custom_call_target="tpu_custom_call" | custom-call | tf_op jit(solution)/shard_map/term/pallas_call | solution.py:296
  50.0 6.1 %collective-permute-start = (bf16[64,576]{1,0:T(8,128)(2,1)S(1)}, bf16[64,576]{1,0:T(8,128)(2,1)S(1)}, u32[]{:S(2)}, u32[]{:S(2)}) collective-permute-start(bf16[64,576]{1,0:T(8,128)(2,1)S(1)} %get-tuple-element.16), channel_id=1, source_target_pairs={{0,2},{1,3},{2,0},{3,1},{4,6},{5,7},{6,4},{7,5},{8,10},{9,11},{10,... | collective-permute-start | bytes 221192 | tf_op jit(solution)/shard_map/ppermute | solution.py:346
  56.1 1.2 %collective-permute-start.1 = (bf16[64,576]{1,0:T(8,128)(2,1)S(1)}, bf16[64,576]{1,0:T(8,128)(2,1)S(1)}, u32[]{:S(2)}, u32[]{:S(2)}) collective-permute-start(bf16[64,576]{1,0:T(8,128)(2,1)S(1)} %get-tuple-element.17), channel_id=1, source_target_pairs={{0,1},{1,2},{2,3},{3,0},{4,5},{5,6},{6,7},{7,4},{8,9},{9,10},{10,1... | collective-permute-start | bytes 221192 | tf_op jit(solution)/shard_map/ppermute | solution.py:346
  57.3 2.4 %collective-permute-start.2 = (bf16[64,576]{1,0:T(8,128)(2,1)S(1)}, bf16[64,576]{1,0:T(8,128)(2,1)S(1)}, u32[]{:S(2)}, u32[]{:S(2)}) collective-permute-start(bf16[64,576]{1,0:T(8,128)(2,1)S(1)} %get-tuple-element.18), channel_id=1, source_target_pairs={{0,3},{1,0},{2,1},{3,2},{4,7},{5,4},{6,5},{7,6},{8,11},{9,8},{10,9... | collective-permute-start | bytes 221192 | tf_op jit(solution)/shard_map/ppermute | solution.py:346
  59.6 0.0 collective-permute-done.refs_0_
  59.6 4.5 %collective-permute-done.1.refs_1_ = bf16[64,576]{1,0:T(8,128)(2,1)S(1)} collective-permute-done((bf16[64,576]{1,0:T(8,128)(2,1)S(1)}, bf16[64,576]{1,0:T(8,128)(2,1)S(1)}, u32[]{:S(2)}, u32[]{:S(2)}) %collective-permute-start.1) | collective-permute-done | bytes 73760 | tf_op jit(solution)/shard_map/ppermute | solution.py:346
  64.2 0.0 collective-permute-done.2.refs_2_
  64.2 1.1 %finish.1 = f32[10,3,6,384]{3,2,1,0:T(8,128)} custom-call(bf16[192,384]{1,0:T(8,128)(2,1)S(1)} %get-tuple-element.12.fold_ref, f32[10,3,6,384]{3,2,1,0:T(8,128)S(1)} %get-tuple-element.13.scale_ref, f32[80,1152]{1,0:T(8,128)S(1)} %get-tuple-element.15.own_ref, bf16[64,576]{1,0:T(8,128)(2,1)S(1)} %collective-permute-done.refs_0_, ...), custom_call_target="tpu_custom_call" | custom-call | tf_op jit(solution)/shard_map/finish/pallas_call | solution.py:329
  (2 shorter events, 0.0 us)
Async XLA Ops:
  3.9 10.6 %copy-start.2 = (s32[384]{0:T(512)S(1)}, s32[384]{0:T(512)}, u32[]{:S(2)}) copy-start(s32[384]{0:T(512)} %vir_ref.3) | copy-start | bytes 4612
  3.9 10.6 %copy-start.3 = (f32[384]{0:T(512)S(1)}, f32[384]{0:T(512)}, u32[]{:S(2)}) copy-start(f32[384]{0:T(512)} %vir_e_ref.1) | copy-start | bytes 4612
  4.0 10.6 %copy-start.4 = (s32[40]{0:T(128)S(1)}, s32[40]{0:T(128)}, u32[]{:S(2)}) copy-start(s32[40]{0:T(128)} %occ_ref.3) | copy-start | bytes 484
  4.0 10.6 %copy-start.5 = (f32[40]{0:T(128)S(1)}, f32[40]{0:T(128)}, u32[]{:S(2)}) copy-start(f32[40]{0:T(128)} %occ_e_ref.1) | copy-start | bytes 484
  4.0 38.7 %all-to-all-start = ((bf16[64,120,128]{2,1,0:T(8,128)(2,1)}), bf16[64,120,128]{2,1,0:T(8,128)(2,1)S(1)}, u32[]{:S(2)}, u32[]{:S(2)}) async-start(bf16[64,120,128]{2,1,0:T(8,128)(2,1)} %pack.1), calls=%async_computation | async-start | bytes 3932160 | tf_op jit(solution)/shard_map/all_to_all | solution.py:341
  14.5 3.5 %copy-start = (bf16[40,96,3,384]{3,1,2,0:T(8,128)(2,1)S(1)}, bf16[40,96,3,384]{3,1,2,0:T(8,128)(2,1)}, u32[]{:S(2)}) copy-start(bf16[40,96,3,384]{3,1,2,0:T(8,128)(2,1)} %param.7) | copy-start | bytes 26542084
  20.7 3.4 %copy-start.1 = (bf16[3840,1152]{1,0:T(8,128)(2,1)}, bf16[3840,1152]{1,0:T(8,128)(2,1)S(1)}, u32[]{:S(2)}) copy-start(bf16[3840,1152]{1,0:T(8,128)(2,1)S(1)} %get-tuple-element.14.w_hbm) | copy-start | bytes 26542084
  50.0 9.7 %collective-permute-start = (bf16[64,576]{1,0:T(8,128)(2,1)S(1)}, bf16[64,576]{1,0:T(8,128)(2,1)S(1)}, u32[]{:S(2)}, u32[]{:S(2)}) collective-permute-start(bf16[64,576]{1,0:T(8,128)(2,1)S(1)} %get-tuple-element.16), channel_id=1, source_target_pairs={{0,2},{1,3},{2,0},{3,1},{4,6},{5,7},{6,4},{7,5},{8,10},{9,11},{10,... | collective-permute-start | bytes 221192 | tf_op jit(solution)/shard_map/ppermute | solution.py:346
  56.1 8.1 %collective-permute-start.1 = (bf16[64,576]{1,0:T(8,128)(2,1)S(1)}, bf16[64,576]{1,0:T(8,128)(2,1)S(1)}, u32[]{:S(2)}, u32[]{:S(2)}) collective-permute-start(bf16[64,576]{1,0:T(8,128)(2,1)S(1)} %get-tuple-element.17), channel_id=1, source_target_pairs={{0,1},{1,2},{2,3},{3,0},{4,5},{5,6},{6,7},{7,4},{8,9},{9,10},{10,1... | collective-permute-start | bytes 221192 | tf_op jit(solution)/shard_map/ppermute | solution.py:346
  57.3 6.9 %collective-permute-start.2 = (bf16[64,576]{1,0:T(8,128)(2,1)S(1)}, bf16[64,576]{1,0:T(8,128)(2,1)S(1)}, u32[]{:S(2)}, u32[]{:S(2)}) collective-permute-start(bf16[64,576]{1,0:T(8,128)(2,1)S(1)} %get-tuple-element.18), channel_id=1, source_target_pairs={{0,3},{1,0},{2,1},{3,2},{4,7},{5,4},{6,5},{7,6},{8,11},{9,8},{10,9... | collective-permute-start | bytes 221192 | tf_op jit(solution)/shard_map/ppermute | solution.py:346

commit v5 on v4

--- a/solution.py
+++ b/solution.py
@@ -26,8 +26,8 @@
 
 COUPLES = 13
 TILES = 20
-GROUPS = 5
 ROWS = 120
+CHUNK = 288
 A_WIDTH, B_WIDTH = 64, 32
 BLOCK = 1280
 STEPS = OCC * CW // BLOCK
@@ -37,22 +37,14 @@
     return lax.dot_general(x, y, (((1,), (1,)), ((), ())), preferred_element_type=F32)
 
 
-def pack_kernel(x_hbm, out_hbm, main_ref, rest_ref, pick_ref, out_ref, sem, out_sem):
+def pack_kernel(x_hbm, out_hbm, x_ref, tile_ref, pick_ref, out_ref, sem, out_sem):
     me = lax.axis_index("grp")
     odd, phase = lax.rem(me, 2), lax.rem(me, 4)
-    for t in range(TILES):
-        n, j = divmod(t, 4)
-        dst = rest_ref if j == 3 else main_ref.at[j]
-        for p in range(2 if t < COUPLES else 4):
-            if t < COUPLES:
-                pair, first_c, width = 2 * t + p - odd, 0, A_WIDTH
-            else:
-                pair, first_c, width = 4 * (t - COUPLES) + p - phase, A_WIDTH, B_WIDTH
-            pltpu.make_async_copy(
-                x_hbm.at[jnp.clip(pair, 0, PAIR - 1), pl.ds(first_c, width)],
-                dst.at[pl.ds(n * 128 + p * width, width)],
-                sem,
-            ).start()
+    arrivals = []
+    for step, (first, last, first_c, last_c) in enumerate(PIECES):
+        part = (pl.ds(first, last - first), pl.ds(first_c, last_c - first_c))
+        arrivals.append(pltpu.make_async_copy(x_hbm.at[part], x_ref.at[part], sem.at[step]))
+        arrivals[-1].start()
     row = lax.broadcasted_iota(jnp.int32, (GRP * 4, 1), 0)
     dest, sub = row // 8, row % 8
     col = lax.broadcasted_iota(jnp.int32, (GRP * 4, 256), 1)
@@ -66,19 +58,43 @@
         for j in range(3):
             pick_ref[half, j, :, :256] = main
             pick_ref[half, j, :, 256:] = pick(jnp.where(sub >= 6, first + 2 * j + sub - 6, -1))
-    pltpu.make_async_copy(main_ref, main_ref, sem).wait()
-    pltpu.make_async_copy(rest_ref, rest_ref, sem).wait()
-    for j in range(3):
-        for half in range(2):
-            lanes = slice(128 * half, 128 * half + 256)
-            both = jnp.concatenate([main_ref[j, :, lanes], rest_ref[:, lanes]], 1)
-            value = nt_dot(pick_ref[half, j], both).astype(BF16)
-            for n in range(GROUPS):
-                tile = value[:, n * 128 : n * 128 + 128].reshape(GRP // 2, 8, 128)
-                out_ref[j, half * 32 : half * 32 + 32, n * 8 : n * 8 + 8, :] = tile
-        pltpu.make_async_copy(out_ref.at[j], out_hbm.at[:, pl.ds(40 * j, 40)], out_sem.at[j]).start()
-    for j in range(3):
-        pltpu.make_async_copy(out_ref.at[j], out_hbm.at[:, pl.ds(40 * j, 40)], out_sem.at[j]).wait()
+
+    def place(t, at):
+        for p in range(2 if t < COUPLES else 4):
+            if t < COUPLES:
+                pair, first_c, width = 2 * t + p - odd, 0, A_WIDTH
+            else:
+                pair, first_c, width = 4 * (t - COUPLES) + p - phase, A_WIDTH, B_WIDTH
+            source = x_ref[jnp.clip(pair, 0, PAIR - 1), first_c : first_c + width, :]
+            tile_ref[at + p * width : at + (p + 1) * width, :] = source
+
+    sends = []
+    for step, groups in enumerate(PACK_STEPS):
+        if step < len(arrivals):
+            arrivals[step].wait()
+        size = 128 * len(groups)
+        for n, group in enumerate(groups):
+            for j in range(4):
+                place(4 * group + j, (4 * step + j) * 256 + n * 128)
+        for j in range(3):
+            main, rest = (slice((4 * step + m) * 256, (4 * step + m) * 256 + size) for m in (j, 3))
+            for half in range(2):
+                lanes = slice(128 * half, 128 * half + 256)
+                both = jnp.concatenate([tile_ref[main, lanes], tile_ref[rest, lanes]], 1)
+                value = nt_dot(pick_ref[half, j], both).astype(BF16)
+                for n, group in enumerate(groups):
+                    tile = value[:, n * 128 : n * 128 + 128].reshape(GRP // 2, 8, 128)
+                    at = (3 * group + j) * 8
+                    out_ref[half * 32 : half * 32 + 32, at : at + 8, :] = tile
+        rows = pl.ds(24 * groups[0], 24 * len(groups))
+        sends.append(pltpu.make_async_copy(out_ref.at[:, rows], out_hbm.at[:, rows], out_sem.at[step]))
+        sends[-1].start()
+    for send in sends:
+        send.wait()
+
+
+PACK_STEPS = ((0,), (1, 2), (3, 4))
+PIECES = ((0, 8, 0, A_WIDTH), (8, PAIR, 0, A_WIDTH), (0, PAIR, A_WIDTH, CW))
 
 
 def pack(x):
@@ -88,12 +104,12 @@
         in_specs=[HBM],
         out_specs=HBM,
         scratch_shapes=[
-            pltpu.VMEM((3, GROUPS * 128, VIR), BF16),
-            pltpu.VMEM((GROUPS * 128, VIR), BF16),
+            pltpu.VMEM((PAIR, CW, VIR), BF16),
+            pltpu.VMEM((len(PACK_STEPS) * 4 * 256, VIR), BF16),
             pltpu.VMEM((2, 3, GRP * 4, 512), BF16),
-            pltpu.VMEM((3, GRP, 40, 128), BF16),
-            pltpu.SemaphoreType.DMA,
-            pltpu.SemaphoreType.DMA((3,)),
+            pltpu.VMEM((GRP, ROWS, 128), BF16),
+            pltpu.SemaphoreType.DMA((len(PIECES),)),
+            pltpu.SemaphoreType.DMA((len(PACK_STEPS),)),
         ],
         compiler_params=pltpu.CompilerParams(vmem_limit_bytes=62 * MIB),
         name="pack",
@@ -182,9 +198,9 @@
     for t in range(TILES):
         n, j = divmod(t, 4)
         if j < 3:
-            tiles.append(got[GROUPS * j + n])
+            tiles.append(got[3 * n + j])
         else:
-            a, b, c = (pltpu.roll(got[GROUPS * j + n], 2 + 2 * j, 0) for j in range(3))
+            a, b, c = (pltpu.roll(got[3 * n + j], 2 + 2 * j, 0) for j in range(3))
             tiles.append(jnp.where(sub < 2, a, jnp.where(sub < 4, b, c)))
     return tiles
 
@@ -287,15 +303,19 @@
                 masked_ref[at : at + 8, :] = jnp.where(keep, sum_ref[rows, j * VIR : (j + 1) * VIR], 0.0)
         if s > 0:
             folded = nt_dot(masked_ref[...].astype(BF16), fold_ref[...]).astype(BF16)
+            ends = []
             for j in range(OJW):
                 chunk = jnp.dot(dense, folded[j * OWN * 8 : (j + 1) * OWN * 8], preferred_element_type=F32)
-                outs[s - 1][:, j * SLOT : (j + 1) * SLOT] = chunk.astype(BF16)
+                outs[s - 1][64 * j : 64 * j + 64, :] = chunk[:, :128].astype(BF16)
+                ends.append(chunk[:, 128:])
+            outs[s - 1][192:256, :] = jnp.concatenate(ends[:2], 1).astype(BF16)
+            outs[s - 1][256:, :] = jnp.concatenate([ends[2][:32], ends[2][32:]], 1).astype(BF16)
 
 
 def term(occ_irrep, vir_irrep, got, fold, w):
     return pl.pallas_call(
         term_kernel,
-        out_shape=[jax.ShapeDtypeStruct((64, OJW * SLOT), BF16)] * 3
+        out_shape=[jax.ShapeDtypeStruct((CHUNK, 128), BF16)] * 3
         + [jax.ShapeDtypeStruct((OWN * 8, WIDE), F32)],
         in_specs=[SMEM, SMEM] + [VMEM] * 3 + [HBM],
         out_specs=[VMEM] * 4,
@@ -313,11 +333,18 @@
     )(occ_irrep, vir_irrep, vir_irrep.reshape(1, VIR), got, fold, w)
 
 
+def unpacked(chunk, j):
+    if j < 2:
+        end = chunk[192:256, 64 * j : 64 * j + 64]
+    else:
+        end = jnp.concatenate([chunk[256:, :64], chunk[256:, 64:]], 0)
+    return jnp.concatenate([chunk[64 * j : 64 * j + 64, :], end], 1)
+
+
 def finish_kernel(fold_ref, scale_ref, own_ref, *refs):
     chunks, out_ref = refs[:3], refs[3]
     for j in range(OJW):
-        lanes = slice(j * SLOT, (j + 1) * SLOT)
-        stacked = jnp.concatenate([chunk[:, lanes] for chunk in chunks], 0)
+        stacked = jnp.concatenate([unpacked(chunk, j) for chunk in chunks], 0)
         parts = jnp.dot(stacked, fold_ref[...], preferred_element_type=F32)
         total = parts[:64] + parts[64:128] + parts[128:]
         for i in range(OWN):
@@ -343,7 +370,7 @@
         occ_irrep, vir_irrep, occ_energy, vir_energy, jnp.swapaxes(integrals, 1, 2)
     )
     *chunks, own = term(occ_irrep, vir_irrep, got, fold, w)
-    arrived = [lax.ppermute(chunks[s - 1], "con", [(n, (n + s) % CON) for n in range(CON)]) for s in (2, 1, 3)]
+    arrived = [lax.ppermute(chunks[s - 1], "con", [(n, (n + s) % CON) for n in range(CON)]) for s in (1, 3, 2)]
     return finish(fold, scale, own, arrived)
 
 

time: 65.6 us -> 64.7 us (0.986); the launches traced: 65.2 us -> 63.7 us
  waiting for transfers between devices: 23.1 us -> 21.6 us
    ppermute x3, waiting for transfers between devices: 4.52 us -> 3.03 us  [shards(): lax.ppermute(chunks[s - 1], 'con', [(n, (n + s) % CON) for n in range(CON)])]
where the time goes in v5:
time: 64.7 us; the launch traced here: 63.7 us
  waiting for transfers between devices  21.6 us (33%)
  starting transfers between devices  20.1 us (31%)
  Pallas kernels  14.9 us (23%)
  local copies, waits for them, and re-layouts  6.95 us (11%)
    all_to_all x1, waiting for transfers between devices, shards(): got = lax.all_to_all(sent, 'grp', split_axis=0, concat_axis=0, tiled=True)  18.6 us
    all_to_all x1, starting transfers between devices, shards(): got = lax.all_to_all(sent, 'grp', split_axis=0, concat_axis=0, tiled=True)  10.5 us
    ppermute x3, starting transfers between devices, shards(): lax.ppermute(chunks[s - 1], 'con', [(n, (n + s) % CON) for n in range(CON)])  9.66 us
    pallas_call x1, Pallas kernels, term(): pl.pallas_call(term_kernel, out_shape=[jax.ShapeDtypeStruct((CHUNK, 128),...  7.32 us
    unnamed x12, local copies, waits for them, and re-layouts  6.94 us
    pallas_call x1, Pallas kernels, pack(): pl.pallas_call(pack_kernel, out_shape=jax.ShapeDtypeStruct((GRP, ROWS, 12...  3.87 us
    ppermute x3, waiting for transfers between devices, shards(): lax.ppermute(chunks[s - 1], 'con', [(n, (n + s) % CON) for n in range(CON)])  3.03 us
    pallas_call x1, Pallas kernels, prepare(): pl.pallas_call(prepare_kernel, out_shape=[jax.ShapeDtypeStruct((OCC * CW,...  2.62 us
  transfers between devices with their start and end apart: 4, of which 2 were waited for; matrix products, arithmetic and copies ran while one was open for 0% of the time, Pallas kernels for 4%

profile of v5, /device:TPU:1, one launch (start us, length us, event | category | flops | bytes accessed | tf_op | source)
XLA Modules:
  0.0 63.7 jit_solution(4967822872795629586)
XLA Ops:
  0.0 3.9 %pack.1 = bf16[64,120,128]{2,1,0:T(8,128)(2,1)} custom-call(bf16[25,96,384]{2,1,0:T(8,128)(2,1)} %bitcast.3), custom_call_target="tpu_custom_call" | custom-call | tf_op jit(solution)/shard_map/pack/pallas_call | solution.py:101
  3.9 0.0 copy-start.2
  3.9 0.0 copy-start.3
  3.9 0.0 copy-start.4
  3.9 0.0 copy-start.5
  3.9 10.5 %all-to-all-start = ((bf16[64,120,128]{2,1,0:T(8,128)(2,1)}), bf16[64,120,128]{2,1,0:T(8,128)(2,1)S(1)}, u32[]{:S(2)}, u32[]{:S(2)}) async-start(bf16[64,120,128]{2,1,0:T(8,128)(2,1)} %pack.1), calls=%async_computation | async-start | bytes 3932160 | tf_op jit(solution)/shard_map/all_to_all | solution.py:368
  14.4 0.0 copy-done.2
  14.4 0.0 copy-done.3
  14.5 0.0 copy-done.4
  14.5 0.0 copy-done.5
  14.5 0.0 copy-start
  14.5 3.5 %copy-done = bf16[40,96,3,384]{3,1,2,0:T(8,128)(2,1)S(1)} copy-done((bf16[40,96,3,384]{3,1,2,0:T(8,128)(2,1)S(1)}, bf16[40,96,3,384]{3,1,2,0:T(8,128)(2,1)}, u32[]{:S(2)}) %copy-start) | copy-done | bytes 8847384
  18.0 2.6 %prepare.1 = (bf16[3840,1152]{1,0:T(8,128)(2,1)S(1)}, bf16[192,384]{1,0:T(8,128)(2,1)S(1)}, f32[10,3,6,384]{3,2,1,0:T(8,128)S(1)}) custom-call(s32[40]{0:T(128)S(1)} %copy-done.4, s32[384]{0:T(512)S(1)} %copy-done.2, f32[40]{0:T(128)S(1)} %copy-done.5, f32[384]{0:T(512)S(1)} %copy-done.3, s32[1,384]{1,0:T(1,128)S(1)} %reshape.7.label_ref, ...), custom_call_target="tpu_custom_call" | custom-call | flops 100000000 | bytes 20000000 | tf_op jit(solution)/shard_map/prepare/pallas_call | solution.py:170
  20.6 0.0 copy-start.1
  20.6 3.4 %copy-done.1 = bf16[3840,1152]{1,0:T(8,128)(2,1)} copy-done((bf16[3840,1152]{1,0:T(8,128)(2,1)}, bf16[3840,1152]{1,0:T(8,128)(2,1)S(1)}, u32[]{:S(2)}) %copy-start.1) | copy-done | bytes 8847384
  24.0 18.6 %all-to-all-done.got_ref = bf16[64,120,128]{2,1,0:T(8,128)(2,1)S(1)} async-done(((bf16[64,120,128]{2,1,0:T(8,128)(2,1)}), bf16[64,120,128]{2,1,0:T(8,128)(2,1)S(1)}, u32[]{:S(2)}, u32[]{:S(2)}) %all-to-all-start) | async-done | bytes 1966112 | tf_op jit(solution)/shard_map/all_to_all | solution.py:368
  42.6 7.3 %term.1 = (bf16[288,128]{1,0:T(8,128)(2,1)S(1)}, bf16[288,128]{1,0:T(8,128)(2,1)S(1)}, bf16[288,128]{1,0:T(8,128)(2,1)S(1)}, f32[80,1152]{1,0:T(8,128)S(1)}) custom-call(s32[40]{0:T(128)S(1)} %copy-done.4, s32[384]{0:T(512)S(1)} %copy-done.2, s32[1,384]{1,0:T(1,128)S(1)} %reshape.7.label_ref, bf16[64,120,128]{2,1,0:T(8,128)(2,1)S(1)} %all-to-all-done.got_ref, ...), custom_call_target="tpu_custom_call" | custom-call | tf_op jit(solution)/shard_map/term/pallas_call | solution.py:316
  49.9 3.1 %collective-permute-start = (bf16[288,128]{1,0:T(8,128)(2,1)S(1)}, bf16[288,128]{1,0:T(8,128)(2,1)S(1)}, u32[]{:S(2)}, u32[]{:S(2)}) collective-permute-start(bf16[288,128]{1,0:T(8,128)(2,1)S(1)} %get-tuple-element.16), channel_id=1, source_target_pairs={{0,1},{1,2},{2,3},{3,0},{4,5},{5,6},{6,7},{7,4},{8,9},{9,10},{10,1... | collective-permute-start | bytes 221192 | tf_op jit(solution)/shard_map/ppermute | solution.py:373
  53.0 2.2 %collective-permute-start.1 = (bf16[288,128]{1,0:T(8,128)(2,1)S(1)}, bf16[288,128]{1,0:T(8,128)(2,1)S(1)}, u32[]{:S(2)}, u32[]{:S(2)}) collective-permute-start(bf16[288,128]{1,0:T(8,128)(2,1)S(1)} %get-tuple-element.17), channel_id=1, source_target_pairs={{0,3},{1,0},{2,1},{3,2},{4,7},{5,4},{6,5},{7,6},{8,11},{9,8},{10,9... | collective-permute-start | bytes 221192 | tf_op jit(solution)/shard_map/ppermute | solution.py:373
  55.2 4.4 %collective-permute-start.2 = (bf16[288,128]{1,0:T(8,128)(2,1)S(1)}, bf16[288,128]{1,0:T(8,128)(2,1)S(1)}, u32[]{:S(2)}, u32[]{:S(2)}) collective-permute-start(bf16[288,128]{1,0:T(8,128)(2,1)S(1)} %get-tuple-element.18), channel_id=1, source_target_pairs={{0,2},{1,3},{2,0},{3,1},{4,6},{5,7},{6,4},{7,5},{8,10},{9,11},{10,... | collective-permute-start | bytes 221192 | tf_op jit(solution)/shard_map/ppermute | solution.py:373
  59.6 0.0 collective-permute-done.refs_0_
  59.6 0.0 collective-permute-done.1.refs_1_
  59.6 3.0 %collective-permute-done.2.refs_2_ = bf16[288,128]{1,0:T(8,128)(2,1)S(1)} collective-permute-done((bf16[288,128]{1,0:T(8,128)(2,1)S(1)}, bf16[288,128]{1,0:T(8,128)(2,1)S(1)}, u32[]{:S(2)}, u32[]{:S(2)}) %collective-permute-start.2) | collective-permute-done | bytes 73760 | tf_op jit(solution)/shard_map/ppermute | solution.py:373
  62.6 1.1 %finish.1 = f32[10,3,6,384]{3,2,1,0:T(8,128)} custom-call(bf16[192,384]{1,0:T(8,128)(2,1)S(1)} %get-tuple-element.12.fold_ref, f32[10,3,6,384]{3,2,1,0:T(8,128)S(1)} %get-tuple-element.13.scale_ref, f32[80,1152]{1,0:T(8,128)S(1)} %get-tuple-element.15.own_ref, bf16[288,128]{1,0:T(8,128)(2,1)S(1)} %collective-permute-done.refs_0_, ...), custom_call_target="tpu_custom_call" | custom-call | tf_op jit(solution)/shard_map/finish/pallas_call | solution.py:356
  (2 shorter events, 0.0 us)
Async XLA Ops:
  3.9 10.5 %copy-start.2 = (s32[384]{0:T(512)S(1)}, s32[384]{0:T(512)}, u32[]{:S(2)}) copy-start(s32[384]{0:T(512)} %vir_ref.3) | copy-start | bytes 4612
  3.9 10.5 %copy-start.3 = (f32[384]{0:T(512)S(1)}, f32[384]{0:T(512)}, u32[]{:S(2)}) copy-start(f32[384]{0:T(512)} %vir_e_ref.1) | copy-start | bytes 4612
  3.9 10.6 %copy-start.4 = (s32[40]{0:T(128)S(1)}, s32[40]{0:T(128)}, u32[]{:S(2)}) copy-start(s32[40]{0:T(128)} %occ_ref.3) | copy-start | bytes 484
  3.9 10.6 %copy-start.5 = (f32[40]{0:T(128)S(1)}, f32[40]{0:T(128)}, u32[]{:S(2)}) copy-start(f32[40]{0:T(128)} %occ_e_ref.1) | copy-start | bytes 484
  3.9 38.7 %all-to-all-start = ((bf16[64,120,128]{2,1,0:T(8,128)(2,1)}), bf16[64,120,128]{2,1,0:T(8,128)(2,1)S(1)}, u32[]{:S(2)}, u32[]{:S(2)}) async-start(bf16[64,120,128]{2,1,0:T(8,128)(2,1)} %pack.1), calls=%async_computation | async-start | bytes 3932160 | tf_op jit(solution)/shard_map/all_to_all | solution.py:368
  14.5 3.5 %copy-start = (bf16[40,96,3,384]{3,1,2,0:T(8,128)(2,1)S(1)}, bf16[40,96,3,384]{3,1,2,0:T(8,128)(2,1)}, u32[]{:S(2)}) copy-start(bf16[40,96,3,384]{3,1,2,0:T(8,128)(2,1)} %param.7) | copy-start | bytes 26542084
  20.6 3.4 %copy-start.1 = (bf16[3840,1152]{1,0:T(8,128)(2,1)}, bf16[3840,1152]{1,0:T(8,128)(2,1)S(1)}, u32[]{:S(2)}) copy-start(bf16[3840,1152]{1,0:T(8,128)(2,1)S(1)} %get-tuple-element.14.w_hbm) | copy-start | bytes 26542084
  49.9 9.7 %collective-permute-start = (bf16[288,128]{1,0:T(8,128)(2,1)S(1)}, bf16[288,128]{1,0:T(8,128)(2,1)S(1)}, u32[]{:S(2)}, u32[]{:S(2)}) collective-permute-start(bf16[288,128]{1,0:T(8,128)(2,1)S(1)} %get-tuple-element.16), channel_id=1, source_target_pairs={{0,1},{1,2},{2,3},{3,0},{4,5},{5,6},{6,7},{7,4},{8,9},{9,10},{10,1... | collective-permute-start | bytes 221192 | tf_op jit(solution)/shard_map/ppermute | solution.py:373
  53.0 6.6 %collective-permute-start.1 = (bf16[288,128]{1,0:T(8,128)(2,1)S(1)}, bf16[288,128]{1,0:T(8,128)(2,1)S(1)}, u32[]{:S(2)}, u32[]{:S(2)}) collective-permute-start(bf16[288,128]{1,0:T(8,128)(2,1)S(1)} %get-tuple-element.17), channel_id=1, source_target_pairs={{0,3},{1,0},{2,1},{3,2},{4,7},{5,4},{6,5},{7,6},{8,11},{9,8},{10,9... | collective-permute-start | bytes 221192 | tf_op jit(solution)/shard_map/ppermute | solution.py:373
  55.2 7.4 %collective-permute-start.2 = (bf16[288,128]{1,0:T(8,128)(2,1)S(1)}, bf16[288,128]{1,0:T(8,128)(2,1)S(1)}, u32[]{:S(2)}, u32[]{:S(2)}) collective-permute-start(bf16[288,128]{1,0:T(8,128)(2,1)S(1)} %get-tuple-element.18), channel_id=1, source_target_pairs={{0,2},{1,3},{2,0},{3,1},{4,6},{5,7},{6,4},{7,5},{8,10},{9,11},{10,... | collective-permute-start | bytes 221192 | tf_op jit(solution)/shard_map/ppermute | solution.py:373
